TPU v7x, 1024 devices: a whole 8x8x8 slice. The times are simulated.
1024 devices in a mesh: gx: 16 (over z, core), gy: 64 (over x, y).
Axes of the slice: x: 8, y: 8, z: 8, core: 2. Of those that a mesh axis runs over, the one named last changes fastest.
Arguments:
- initial_state: float32 [9, 4, 64, 8192], P(None, None, 'gx', 'gy'), may hold values from -6 to 6
- lame_lambda: float32 [4, 64, 8192], P(None, 'gx', 'gy'), may hold values from 0.5 to 1.5
- shear_modulus: float32 [4, 64, 8192], P(None, 'gx', 'gy'), may hold values from 0.3 to 1
- buoyancy: float32 [4, 64, 8192], P(None, 'gx', 'gy'), may hold values from 0.5 to 1
- source_cells: int32 [65536], P(('gx', 'gy')), may hold values from 0 to 2047
- source_wavelet: float32 [3, 65536], P(None, ('gx', 'gy')), may hold values from -8 to 8
- segment_start: int32 [2097152], P(('gx', 'gy')), may hold values from 0 to 1935
- segment_weight: float32 [2, 2097152], P(None, ('gx', 'gy')), may hold values from 0.2 to 1
- partial_owner: int32 [2097152, 1], P(('gx', 'gy')), may hold values from 0 to 1023; in each aligned block of 2048 rows (0 to 2047, 2048 to 4095, ...) at most 4 rows name the same one
- partial_channel: int32 [2097152], P(('gx', 'gy')), may hold values from 0 to 1023
- observed_data: float32 [3, 1048576], P(None, ('gx', 'gy')), may hold values from -6 to 6
Outputs:
- residuals: float32 [3, 1048576], P(None, ('gx', 'gy'))
- gradients: float32 [2, 4, 64, 8192], P(None, None, 'gx', 'gy')
Inputs may be any that keep to these rules, and one draw needn't show every extreme that they name: `partial_owner`: each row names the device that owns the segment's channel, counted with gx slowest; the rows of one device name one owner at most 4 times. `partial_channel`: the segment's channel among its owner's 1024 channels. `segment_start`: index of the segment's first cell in its device's grid of starts of shape [4, 4, 121], flattened in that order. `source_cells`: index of the source's cell in its device's tile of shape [4, 4, 128], flattened in that order; cells may repeat.
All inputs are finite; a program needn't handle non-finite values.
Results may differ from a plain program's by a relative error of at most 0.00002.
Values sent between devices are 32-bit elements; how exact they have to be, the bound alone decides.
A program may use at most 32 MiB of HBM per device.

v0:
```python
import jax
import jax.numpy as jnp
from jax import lax
from jax.sharding import PartitionSpec as P

GAUGE = 8


time_step = 0.25


def extended(x, sides, width):
    for axis, dim in sides:
        count, length = (lax.axis_size(axis), x.shape[dim])
        up = [(i, (i + 1) % count) for i in range(count - 1)]
        down = [(j, i) for i, j in up]
        last = lax.slice_in_dim(x, length - width, length, axis=dim)
        first = lax.slice_in_dim(x, 0, width, axis=dim)
        before = lax.ppermute(last, axis, up)
        after = lax.ppermute(first, axis, down)
        x = jnp.concatenate([before, x, after], axis=dim)
    return x


def crop_rim(values):
    return values[..., 1:-1, 1:-1]


def ahead_x(values):
    return values[..., 2:, 1:-1] - values[..., 1:-1, 1:-1]


def behind_x(values):
    return values[..., 1:-1, 1:-1] - values[..., :-2, 1:-1]


def ahead_y(values):
    return values[..., 1:-1, 2:] - values[..., 1:-1, 1:-1]


def behind_y(values):
    return values[..., 1:-1, 1:-1] - values[..., 1:-1, :-2]


def ahead_z(inner_part):
    return (
        jnp.concatenate(
            [inner_part[..., 1:, :, :], jnp.zeros_like(inner_part[..., :1, :, :])], axis=-3
        )
        - inner_part
    )


def behind_z(inner_part):
    return inner_part - jnp.concatenate(
        [jnp.zeros_like(inner_part[..., :1, :, :]), inner_part[..., :-1, :, :]], axis=-3
    )


def velocity_update(velocity, stress_pad, buoyancy):
    accel_x = ahead_x(stress_pad[0]) + behind_y(stress_pad[3]) + behind_z(crop_rim(stress_pad[4]))
    accel_y = behind_x(stress_pad[3]) + ahead_y(stress_pad[1]) + behind_z(crop_rim(stress_pad[5]))
    accel_z = behind_x(stress_pad[4]) + behind_y(stress_pad[5]) + ahead_z(crop_rim(stress_pad[2]))
    return velocity + time_step * buoyancy * jnp.stack([accel_x, accel_y, accel_z])


def strain_rates(velocity_pad):
    along_x = velocity_pad[0]
    along_y = velocity_pad[1]
    along_z = velocity_pad[2]
    return jnp.stack(
        [
            behind_x(along_x),
            behind_y(along_y),
            behind_z(crop_rim(along_z)),
            ahead_y(along_x) + ahead_x(along_y),
            ahead_z(crop_rim(along_x)) + ahead_x(along_z),
            ahead_z(crop_rim(along_y)) + ahead_y(along_z),
        ]
    )


def stress_update(stress, strains, lame_lambda, shear_modulus):
    dilation = strains[0] + strains[1] + strains[2]
    normal = stress[:3] + time_step * (lame_lambda * dilation + 2.0 * shear_modulus * strains[:3])
    sheared = stress[3:] + time_step * shear_modulus * strains[3:]
    return jnp.concatenate([normal, sheared])


def gradient_terms(forward, adjoint):
    products = forward * adjoint
    lambda_term = (forward[0] + forward[1] + forward[2]) * (adjoint[0] + adjoint[1] + adjoint[2])
    shear_term = (
        2.0 * (products[0] + products[1] + products[2]) + products[3] + products[4] + products[5]
    )
    return jnp.stack([lambda_term, shear_term])


def window_sums(values, gauge_len):
    span_len = values.shape[-1] - gauge_len + 1
    running = values[..., 0:span_len]
    for offset in range(1, gauge_len):
        running = running + values[..., offset : offset + span_len]
    return running


def spread_back(values, gauge_len):
    widths = [(0, 0)] * (values.ndim - 1)
    running = jnp.pad(values, widths + [(0, gauge_len - 1)])
    for offset in range(1, gauge_len):
        running = running + jnp.pad(values, widths + [(offset, gauge_len - 1 - offset)])
    return running


def run_step(velocity, stress, lame_lambda, shear_modulus, buoyancy):
    stress_pad = extended(stress, (("gx", 2), ("gy", 3)), 1)
    velocity = velocity_update(velocity, stress_pad, buoyancy)
    velocity_pad = extended(velocity, (("gx", 2), ("gy", 3)), 1)
    strains = strain_rates(velocity_pad)
    stress = stress_update(stress, strains, lame_lambda, shear_modulus)
    return (velocity, stress, strains)


def shards(
    initial_state,
    lame_lambda,
    shear_modulus,
    buoyancy,
    source_cells,
    source_wavelet,
    segment_start,
    segment_weight,
    partial_owner,
    partial_channel,
    observed_data,
):
    depth_len, rows_x, cols_y = lame_lambda.shape
    steps_count = source_wavelet.shape[0]
    channel_count = observed_data.shape[1]
    part_count = segment_start.shape[0]
    rows_gx = lax.axis_size("gx")
    cols_gy = lax.axis_size("gy")
    devices = rows_gx * cols_gy
    capacity = max(2, 2 * part_count // devices)
    span_local = cols_y - GAUGE + 1
    owners = partial_owner[:, 0]
    sort_order = jnp.argsort(owners, stable=True)
    sorted_owner = owners[sort_order]
    first_pos = jnp.searchsorted(sorted_owner, sorted_owner, side="left")
    slot_rank = (
        jnp.zeros_like(owners)
        .at[sort_order]
        .set(jnp.arange(part_count, dtype=jnp.int32) - first_pos)
    )
    slot_index = owners * capacity + slot_rank
    id_buffer = jnp.zeros((devices * capacity,), jnp.int32).at[slot_index].set(partial_channel)
    incoming_ids = lax.all_to_all(
        lax.all_to_all(
            id_buffer.reshape(rows_gx, cols_gy * capacity),
            "gx",
            split_axis=0,
            concat_axis=0,
            tiled=True,
        ),
        "gy",
        split_axis=1,
        concat_axis=1,
        tiled=True,
    ).reshape(-1)
    velocity = initial_state[:3]
    stress = initial_state[3:]
    forward_strains = []
    partial_rows = []
    for step_index in range(steps_count):
        normal = (
            stress[:3]
            .reshape(3, -1)
            .at[:, source_cells]
            .add(source_wavelet[step_index])
            .reshape(3, depth_len, rows_x, cols_y)
        )
        stress = jnp.concatenate([normal, stress[3:]])
        velocity, stress, strains = run_step(velocity, stress, lame_lambda, shear_modulus, buoyancy)
        forward_strains.append(strains)
        windows = window_sums(strains[:2], GAUGE).reshape(2, -1)[:, segment_start]
        partial_now = segment_weight[0] * windows[0] + segment_weight[1] * windows[1]
        partial_rows.append(partial_now)
    all_buffer = (
        jnp.zeros((devices * capacity, steps_count), jnp.float32)
        .at[slot_index]
        .set(jnp.stack(partial_rows, axis=1))
    )
    arrived = lax.all_to_all(
        lax.all_to_all(
            all_buffer.reshape(rows_gx, cols_gy * capacity * steps_count),
            "gx",
            split_axis=0,
            concat_axis=0,
            tiled=True,
        ),
        "gy",
        split_axis=1,
        concat_axis=1,
        tiled=True,
    )
    arrived = arrived.reshape(devices * capacity, steps_count)
    channel_sums = (
        jnp.zeros((steps_count, channel_count), jnp.float32).at[:, incoming_ids].add(arrived.T)
    )
    residuals = channel_sums - observed_data
    reply = residuals[:, incoming_ids].T.reshape(rows_gx, cols_gy * capacity * steps_count)
    returned = lax.all_to_all(
        lax.all_to_all(reply, "gx", split_axis=0, concat_axis=0, tiled=True),
        "gy",
        split_axis=1,
        concat_axis=1,
        tiled=True,
    )
    returned = returned.reshape(devices * capacity, steps_count)[slot_index]
    adj_velocity = jnp.zeros((3, depth_len, rows_x, cols_y), jnp.float32)
    adj_stress = jnp.zeros((6, depth_len, rows_x, cols_y), jnp.float32)
    gradients = jnp.zeros((2, depth_len, rows_x, cols_y), jnp.float32)
    for turn_index in range(steps_count):
        back_values = returned[:, steps_count - 1 - turn_index]
        load_map = (
            jnp.zeros((2, depth_len * rows_x * span_local), jnp.float32)
            .at[:, segment_start]
            .add(segment_weight * back_values)
        )
        spread = spread_back(load_map.reshape(2, depth_len, rows_x, span_local), GAUGE)
        adj_stress = jnp.concatenate([adj_stress[:2] + spread, adj_stress[2:]])
        adj_velocity, adj_stress, adj_strains = run_step(
            adj_velocity, adj_stress, lame_lambda, shear_modulus, buoyancy
        )
        gradients = gradients + gradient_terms(
            forward_strains[steps_count - 1 - turn_index], adj_strains
        )
    return (residuals, gradients)


def solution(mesh):
    in_specs = (
        P(None, None, "gx", "gy"),
        P(None, "gx", "gy"),
        P(None, "gx", "gy"),
        P(None, "gx", "gy"),
        P(("gx", "gy")),
        P(None, ("gx", "gy")),
        P(("gx", "gy")),
        P(None, ("gx", "gy")),
        P(("gx", "gy"), None),
        P(("gx", "gy")),
        P(None, ("gx", "gy")),
    )
    out_specs = (P(None, ("gx", "gy")), P(None, None, "gx", "gy"))
    return jax.shard_map(shards, mesh=mesh, in_specs=in_specs, out_specs=out_specs, check_vma=False)
```

profile of v0, /device:TPU:9, one launch (start us, length us, event | category | flops | bytes accessed | tf_op | source)
XLA Modules:
  0.0 606.4 jit_solution(15558987988843275827)
XLA Ops:
  7.6 4.8 collective-permute-start
  13.4 5.9 collective-permute-start.3
  21.2 6.7 %collective-permute-done.2 = f32[6,4,6,1]{3,2,1,0:T(8,128)S(1)} collective-permute-done((f32[6,4,6,1]{3,2,1,0:T(8,128)S(1)}, f32[6,4,6,1]{3,2,1,0:T(8,128)S(1)}, u32[]{:S(2)}, u32[]{:S(2)}) %collective-permute-start.2) | collective-permute-done | bytes 608 | tf_op jit(solution)/shard_map/ppermute | solution.py:19
  30.5 6.5 %collective-permute-start.4 = (f32[3,4,1,128]{3,2,1,0:T(1,128)S(1)}, f32[3,4,1,128]{3,2,1,0:T(1,128)S(1)}, u32[]{:S(2)}, u32[]{:S(2)}) collective-permute-start(f32[3,4,1,128]{3,2,1,0:T(1,128)S(1)} %get-tuple-element.288), channel_id=1, source_target_pairs={{0,64},{64,128},{128,192},{192,256},{256,320},{320,384},{384,448},... | collective-permute-start | bytes 18440 | tf_op jit(solution)/shard_map/ppermute | solution.py:19
  39.8 3.4 collective-permute-start.6
  43.6 4.4 collective-permute-done.6
  53.1 5.7 collective-permute-start.8
  58.8 5.0 sort.17
  65.9 3.4 collective-permute-start.10
  69.3 11.8 %gather_fusion.1 = s32[2048]{0:T(1024)S(1)} fusion(s32[2048]{0:T(1024)S(1)} %bitcast.311, s32[2048]{0:T(1024)S(1)} %get-tuple-element.302), kind=kCustom, calls=%fused_computation.1 | custom fusion | bytes 24576 | tf_op jit(solution)/shard_map/gather | solution.py:148
  83.7 3.6 collective-permute-start.12
  87.4 142.4 %while.25 = (s32[]{:T(128)}, u32[2048]{0:T(1024)S(1)}, u32[2048]{0:T(1024)S(1)}, s32[2048]{0:T(1024)S(1)}, s32[]{:T(128)}, /*index=5*/s32[]{:T(128)}, s32[]{}) while((s32[]{:T(128)}, u32[2048]{0:T(1024)S(1)}, u32[2048]{0:T(1024)S(1)}, s32[2048]{0:T(1024)S(1)}, s32[]{:T(128)}, /*index=5*/s32[]{:T(128)}, s32[]{}) %tuple.167), condition=%wide.region_2.3_spmd.clone, body=%wide.region_1.2_spmd.clone.sunk | while | flops 38916 | bytes 135277 | solution.py:149
  87.4 11.8 %gather_fusion = s32[2048]{0:T(1024)S(1)} fusion(s32[2048]{0:T(1024)S(1)} %get-tuple-element.355, u32[2048]{0:T(1024)S(1)} %broadcast_clamp_fusion.6), kind=kCustom, calls=%fused_computation.clone.clone.1 | custom fusion | bytes 24576 | tf_op jit(solution)/shard_map/jit(searchsorted)/jit(_searchsorted_scan_impl)/vmap(jit(_searchsorted_scan_impl))/while/body/eval_jaxpr/gather | solution.py:149
  99.3 11.8 %gather_fusion = s32[2048]{0:T(1024)S(1)} fusion(s32[2048]{0:T(1024)S(1)} %get-tuple-element.355, u32[2048]{0:T(1024)S(1)} %broadcast_clamp_fusion.6), kind=kCustom, calls=%fused_computation.clone.clone.1 | custom fusion | bytes 24576 | tf_op jit(solution)/shard_map/jit(searchsorted)/jit(_searchsorted_scan_impl)/vmap(jit(_searchsorted_scan_impl))/while/body/eval_jaxpr/gather | solution.py:149
  111.1 11.8 %gather_fusion = s32[2048]{0:T(1024)S(1)} fusion(s32[2048]{0:T(1024)S(1)} %get-tuple-element.355, u32[2048]{0:T(1024)S(1)} %broadcast_clamp_fusion.6), kind=kCustom, calls=%fused_computation.clone.clone.1 | custom fusion | bytes 24576 | tf_op jit(solution)/shard_map/jit(searchsorted)/jit(_searchsorted_scan_impl)/vmap(jit(_searchsorted_scan_impl))/while/body/eval_jaxpr/gather | solution.py:149
  123.0 11.8 %gather_fusion = s32[2048]{0:T(1024)S(1)} fusion(s32[2048]{0:T(1024)S(1)} %get-tuple-element.355, u32[2048]{0:T(1024)S(1)} %broadcast_clamp_fusion.6), kind=kCustom, calls=%fused_computation.clone.clone.1 | custom fusion | bytes 24576 | tf_op jit(solution)/shard_map/jit(searchsorted)/jit(_searchsorted_scan_impl)/vmap(jit(_searchsorted_scan_impl))/while/body/eval_jaxpr/gather | solution.py:149
  134.9 11.8 %gather_fusion = s32[2048]{0:T(1024)S(1)} fusion(s32[2048]{0:T(1024)S(1)} %get-tuple-element.355, u32[2048]{0:T(1024)S(1)} %broadcast_clamp_fusion.6), kind=kCustom, calls=%fused_computation.clone.clone.1 | custom fusion | bytes 24576 | tf_op jit(solution)/shard_map/jit(searchsorted)/jit(_searchsorted_scan_impl)/vmap(jit(_searchsorted_scan_impl))/while/body/eval_jaxpr/gather | solution.py:149
  146.7 11.8 %gather_fusion = s32[2048]{0:T(1024)S(1)} fusion(s32[2048]{0:T(1024)S(1)} %get-tuple-element.355, u32[2048]{0:T(1024)S(1)} %broadcast_clamp_fusion.6), kind=kCustom, calls=%fused_computation.clone.clone.1 | custom fusion | bytes 24576 | tf_op jit(solution)/shard_map/jit(searchsorted)/jit(_searchsorted_scan_impl)/vmap(jit(_searchsorted_scan_impl))/while/body/eval_jaxpr/gather | solution.py:149
  158.6 11.8 %gather_fusion = s32[2048]{0:T(1024)S(1)} fusion(s32[2048]{0:T(1024)S(1)} %get-tuple-element.355, u32[2048]{0:T(1024)S(1)} %broadcast_clamp_fusion.6), kind=kCustom, calls=%fused_computation.clone.clone.1 | custom fusion | bytes 24576 | tf_op jit(solution)/shard_map/jit(searchsorted)/jit(_searchsorted_scan_impl)/vmap(jit(_searchsorted_scan_impl))/while/body/eval_jaxpr/gather | solution.py:149
  170.5 11.8 %gather_fusion = s32[2048]{0:T(1024)S(1)} fusion(s32[2048]{0:T(1024)S(1)} %get-tuple-element.355, u32[2048]{0:T(1024)S(1)} %broadcast_clamp_fusion.6), kind=kCustom, calls=%fused_computation.clone.clone.1 | custom fusion | bytes 24576 | tf_op jit(solution)/shard_map/jit(searchsorted)/jit(_searchsorted_scan_impl)/vmap(jit(_searchsorted_scan_impl))/while/body/eval_jaxpr/gather | solution.py:149
  182.3 11.8 %gather_fusion = s32[2048]{0:T(1024)S(1)} fusion(s32[2048]{0:T(1024)S(1)} %get-tuple-element.355, u32[2048]{0:T(1024)S(1)} %broadcast_clamp_fusion.6), kind=kCustom, calls=%fused_computation.clone.clone.1 | custom fusion | bytes 24576 | tf_op jit(solution)/shard_map/jit(searchsorted)/jit(_searchsorted_scan_impl)/vmap(jit(_searchsorted_scan_impl))/while/body/eval_jaxpr/gather | solution.py:149
  194.2 11.8 %gather_fusion = s32[2048]{0:T(1024)S(1)} fusion(s32[2048]{0:T(1024)S(1)} %get-tuple-element.355, u32[2048]{0:T(1024)S(1)} %broadcast_clamp_fusion.6), kind=kCustom, calls=%fused_computation.clone.clone.1 | custom fusion | bytes 24576 | tf_op jit(solution)/shard_map/jit(searchsorted)/jit(_searchsorted_scan_impl)/vmap(jit(_searchsorted_scan_impl))/while/body/eval_jaxpr/gather | solution.py:149
  206.1 11.8 %gather_fusion = s32[2048]{0:T(1024)S(1)} fusion(s32[2048]{0:T(1024)S(1)} %get-tuple-element.355, u32[2048]{0:T(1024)S(1)} %broadcast_clamp_fusion.6), kind=kCustom, calls=%fused_computation.clone.clone.1 | custom fusion | bytes 24576 | tf_op jit(solution)/shard_map/jit(searchsorted)/jit(_searchsorted_scan_impl)/vmap(jit(_searchsorted_scan_impl))/while/body/eval_jaxpr/gather | solution.py:149
  217.9 11.8 %gather_fusion = s32[2048]{0:T(1024)S(1)} fusion(s32[2048]{0:T(1024)S(1)} %get-tuple-element.355, u32[2048]{0:T(1024)S(1)} %broadcast_clamp_fusion.6), kind=kCustom, calls=%fused_computation.clone.clone.1 | custom fusion | bytes 24576 | tf_op jit(solution)/shard_map/jit(searchsorted)/jit(_searchsorted_scan_impl)/vmap(jit(_searchsorted_scan_impl))/while/body/eval_jaxpr/gather | solution.py:149
  229.9 5.2 collective-permute-start.15
  237.1 8.0 %scatter_custom_fusion = s32[2048]{0:T(1024)S(1)} fusion(s32[2048]{0:T(1024)S(1)} %get-tuple-element.303, s32[2048]{0:T(1024)S(1)} %convert_subtract_fusion, s32[]{:T(128)} %constant.51.clone.1), kind=kCustom, calls=%fused_computation.525 | custom fusion | bytes 8196 | tf_op jit(solution)/shard_map/scatter | solution.py:153
  250.6 3.6 collective-permute-start.16
  254.8 8.8 %scatter_custom_fusion.1 = s32[4096]{0:T(1024)} fusion(s32[2048]{0:T(1024)S(1)} %get-tuple-element.308, s32[2048]{0:T(1024)} %param.22, s32[]{:T(128)} %constant.51.clone.1), kind=kCustom, calls=%fused_computation.514 | custom fusion | bytes 16896 | tf_op jit(solution)/shard_map/scatter | solution.py:156
  263.6 14.9 %all-to-all-start = ((s32[16,1,256]{2,1,0:T(1,128)}), s32[16,1,256]{2,1,0:T(1,128)S(1)}, u32[]{:S(2)}, u32[]{:S(2)}) async-start(s32[16,1,256]{2,1,0:T(1,128)} %bitcast.1), calls=%async_computation | async-start | bytes 32768 | tf_op jit(solution)/shard_map/all_to_all | solution.py:158
  278.9 6.7 %collective-permute-start.19 = (f32[6,4,6,1]{3,2,1,0:T(8,128)S(1)}, f32[6,4,6,1]{3,2,1,0:T(8,128)S(1)}, u32[]{:S(2)}, u32[]{:S(2)}) collective-permute-start(f32[6,4,6,1]{3,2,1,0:T(8,128)S(1)} %get-tuple-element.225), channel_id=1, source_target_pairs={{1,0},{2,1},{3,2},{4,3},{5,4},{6,5},{7,6},{8,7},{9,8},{10,9},{11,1... | collective-permute-start | bytes 1736 | tf_op jit(solution)/shard_map/ppermute | solution.py:20
  288.1 5.5 gather_fusion.2
  294.7 10.3 %all-to-all-start.1 = ((s32[16,64,4]{0,2,1:T(4,128)}), s32[16,64,4]{0,2,1:T(4,128)S(1)}, u32[]{:S(2)}, u32[]{:S(2)}) async-start(s32[16,64,4]{0,2,1:T(4,128)} %bitcast.2), calls=%async_computation.1 | async-start | bytes 262144 | tf_op jit(solution)/shard_map/all_to_all | solution.py:157
  308.8 3.4 collective-permute-start.20
  313.1 4.3 collective-permute-start.23
  319.8 5.5 gather_fusion.3
  326.8 5.5 gather_fusion.4
  334.1 6.5 %scatter_custom_fusion.5 = f32[4096,3]{1,0:T(8,128)S(1)} fusion(s32[2048]{0:T(1024)} %copy-done.9, f32[2048,3]{1,0:T(8,128)} %copy.236, f32[]{:T(128)} %constant.50.clone.1), kind=kCustom, calls=%fused_computation.24 | custom fusion | bytes 49664 | tf_op jit(solution)/shard_map/scatter | solution.py:191
  342.7 10.2 %all-to-all-start.2 = ((f32[16,1,768]{2,1,0:T(1,128)}), f32[16,1,768]{2,1,0:T(1,128)S(1)}, u32[]{:S(2)}, u32[]{:S(2)}) async-start(f32[16,1,768]{2,1,0:T(1,128)} %all_to_all.48), calls=%async_computation.2 | async-start | bytes 98304 | tf_op jit(solution)/shard_map/all_to_all | solution.py:194
  353.8 6.5 %all-to-all-done.2 = f32[16,1,768]{2,1,0:T(1,128)S(1)} async-done(((f32[16,1,768]{2,1,0:T(1,128)}), f32[16,1,768]{2,1,0:T(1,128)S(1)}, u32[]{:S(2)}, u32[]{:S(2)}) %all-to-all-start.2) | async-done | bytes 49184 | tf_op jit(solution)/shard_map/all_to_all | solution.py:194
  362.4 10.4 %all-to-all-start.3 = ((f32[64,1,192]{2,1,0:T(1,128)}), f32[64,1,192]{2,1,0:T(1,128)S(1)}, u32[]{:S(2)}, u32[]{:S(2)}) async-start(f32[64,1,192]{2,1,0:T(1,128)} %reshape.435), calls=%async_computation.3 | async-start | bytes 131072 | tf_op jit(solution)/shard_map/all_to_all | solution.py:193
  372.8 6.8 %all-to-all-done.3 = f32[64,1,192]{2,1,0:T(1,128)S(1)} async-done(((f32[64,1,192]{2,1,0:T(1,128)}), f32[64,1,192]{2,1,0:T(1,128)S(1)}, u32[]{:S(2)}, u32[]{:S(2)}) %all-to-all-start.3) | async-done | bytes 49184 | tf_op jit(solution)/shard_map/all_to_all | solution.py:193
  381.9 22.7 %scatter_custom_fusion.6 = f32[3,1024]{0,1:T(8,128)S(1)} fusion(s32[4096]{0:T(1024)S(1)} %bitcast.345, f32[4096,3]{1,0:T(8,128)S(1)} %reshape.251, f32[]{:T(128)} %constant.50.clone.1), kind=kCustom, calls=%fused_computation.32 | custom fusion | flops 12288 | bytes 12292 | tf_op jit(solution)/shard_map/scatter-add | solution.py:208
  404.7 10.8 %gather_fusion.5 = f32[4096,3]{1,0:T(8,128)S(1)} fusion(f32[3,1024]{0,1:T(8,128)S(1)} %sub.387, s32[4096]{0:T(1024)S(1)} %broadcast_clamp_fusion.1), kind=kCustom, calls=%fused_computation.5 | custom fusion | bytes 114688 | tf_op jit(solution)/shard_map/gather | solution.py:211
  417.0 11.4 %all_to_all.56 = f32[16,1,768]{2,1,0:T(1,128)S(1)} all-to-all(f32[16,1,768]{2,1,0:T(1,128)S(1)} %all_to_all.49), channel_id=1, replica_groups=mesh['gx'=16,'gy'=64] {'gx'}, dimensions={0} | all-to-all | bytes 98304 | tf_op jit(solution)/shard_map/all_to_all | solution.py:213
  429.9 15.2 %all_to_all.57 = f32[64,1,192]{2,1,0:T(1,128)S(1)} all-to-all(f32[64,1,192]{2,1,0:T(1,128)S(1)} %reshape.437), channel_id=1, replica_groups=mesh['gx'=16,'gy'=64] {'gy'}, dimensions={0} | all-to-all | bytes 98304 | tf_op jit(solution)/shard_map/all_to_all | solution.py:212
  446.8 5.5 gather_fusion.6
  454.1 11.8 %scatter_custom_fusion.7 = f32[2,1936]{0,1:T(8,128)S(1)} fusion(s32[2048]{0:T(1024)} %get-tuple-element.298, f32[2048,2]{1,0:T(8,128)S(1)} %copy.244, f32[]{:T(128)} %constant.50.clone.1), kind=kCustom, calls=%fused_computation.30 | custom fusion | flops 4096 | bytes 16000 | tf_op jit(solution)/shard_map/scatter-add | solution.py:228
  473.1 4.3 collective-permute-start.27
  479.5 7.1 %collective-permute-done.26 = f32[6,4,6,1]{3,2,1,0:T(8,128)S(1)} collective-permute-done((f32[6,4,6,1]{3,2,1,0:T(8,128)S(1)}, f32[6,4,6,1]{3,2,1,0:T(8,128)S(1)}, u32[]{:S(2)}, u32[]{:S(2)}) %collective-permute-start.26) | collective-permute-done | bytes 608 | tf_op jit(solution)/shard_map/ppermute | solution.py:19
  490.4 3.9 collective-permute-start.28
  497.0 3.4 collective-permute-start.30
  500.8 12.0 %scatter_custom_fusion.8 = f32[2,1936]{0,1:T(8,128)S(1)} fusion(s32[2048]{0:T(1024)} %get-tuple-element.298, f32[2048,2]{1,0:T(8,128)S(1)} %copy.246, f32[]{:T(128)} %constant.50.clone.1), kind=kCustom, calls=%fused_computation.28 | custom fusion | flops 4096 | bytes 16000 | tf_op jit(solution)/shard_map/scatter-add | solution.py:228
  516.4 4.7 collective-permute-start.32
  522.1 5.0 collective-permute-start.35
  529.2 6.6 %collective-permute-done.34 = f32[6,4,6,1]{3,2,1,0:T(8,128)S(1)} collective-permute-done((f32[6,4,6,1]{3,2,1,0:T(8,128)S(1)}, f32[6,4,6,1]{3,2,1,0:T(8,128)S(1)}, u32[]{:S(2)}, u32[]{:S(2)}) %collective-permute-start.34) | collective-permute-done | bytes 608 | tf_op jit(solution)/shard_map/ppermute | solution.py:19
  538.4 5.6 collective-permute-start.36
  546.9 3.4 collective-permute-start.38
  550.7 11.8 %scatter_custom_fusion.9 = f32[2,1936]{0,1:T(8,128)S(1)} fusion(s32[2048]{0:T(1024)} %get-tuple-element.298, f32[2048,2]{1,0:T(8,128)S(1)} %copy.248, f32[]{:T(128)} %constant.50.clone.1), kind=kCustom, calls=%fused_computation.26 | custom fusion | flops 4096 | bytes 16000 | tf_op jit(solution)/shard_map/scatter-add | solution.py:228
  566.1 4.6 collective-permute-start.40
  571.7 5.0 collective-permute-start.43
  578.6 6.7 %collective-permute-done.42 = f32[6,4,6,1]{3,2,1,0:T(8,128)S(1)} collective-permute-done((f32[6,4,6,1]{3,2,1,0:T(8,128)S(1)}, f32[6,4,6,1]{3,2,1,0:T(8,128)S(1)}, u32[]{:S(2)}, u32[]{:S(2)}) %collective-permute-start.42) | collective-permute-done | bytes 608 | tf_op jit(solution)/shard_map/ppermute | solution.py:19
  587.9 5.6 collective-permute-start.44
  596.3 3.4 collective-permute-start.46
  599.7 4.8 collective-permute-done.46
  (386 shorter events, 103.2 us)
Async XLA Ops:
  0.6 20.5 %copy-start.10 = (f32[4,4,128]{2,1,0:T(4,128)S(1)}, f32[4,4,128]{2,1,0:T(4,128)}, u32[]{:S(2)}) copy-start(f32[4,4,128]{2,1,0:T(4,128)} %param.16) | copy-start | bytes 24580
  1.8 26.8 %copy-start.3 = (f32[9,4,4,128]{3,2,1,0:T(4,128)S(1)}, f32[9,4,4,128]{3,2,1,0:T(4,128)}, u32[]{:S(2)}) copy-start(f32[9,4,4,128]{3,2,1,0:T(4,128)} %param.13) | copy-start | bytes 221188
  3.3 39.9 %copy-start.7 = (f32[4,4,128]{2,1,0:T(4,128)S(1)}, f32[4,4,128]{2,1,0:T(4,128)}, u32[]{:S(2)}) copy-start(f32[4,4,128]{2,1,0:T(4,128)} %param.15) | copy-start | bytes 24580
  5.0 43.8 %copy-start.4 = (f32[4,4,128]{2,1,0:T(4,128)S(1)}, f32[4,4,128]{2,1,0:T(4,128)}, u32[]{:S(2)}) copy-start(f32[4,4,128]{2,1,0:T(4,128)} %param.14) | copy-start | bytes 24580
  5.0 7.4 %collective-permute-start.1 = (f32[6,4,1,128]{3,2,1,0:T(1,128)S(1)}, f32[6,4,1,128]{3,2,1,0:T(1,128)S(1)}, u32[]{:S(2)}, u32[]{:S(2)}) collective-permute-start(f32[6,4,1,128]{3,2,1,0:T(1,128)S(1)} %get-tuple-element.259), channel_id=1, source_target_pairs={{64,0},{128,64},{192,128},{256,192},{320,256},{384,320},{448,384},... | collective-permute-start | bytes 36872 | tf_op jit(solution)/shard_map/ppermute | solution.py:20
  7.6 5.6 collective-permute-start
  13.4 7.8 %collective-permute-start.3 = (f32[6,4,6,1]{3,2,1,0:T(8,128)S(1)}, f32[6,4,6,1]{3,2,1,0:T(8,128)S(1)}, u32[]{:S(2)}, u32[]{:S(2)}) collective-permute-start(f32[6,4,6,1]{3,2,1,0:T(8,128)S(1)} %get-tuple-element.235), channel_id=1, source_target_pairs={{1,0},{2,1},{3,2},{4,3},{5,4},{6,5},{7,6},{8,7},{9,8},{10,9},{11,1... | collective-permute-start | bytes 1736 | tf_op jit(solution)/shard_map/ppermute | solution.py:20
  19.2 8.7 %collective-permute-start.2 = (f32[6,4,6,1]{3,2,1,0:T(8,128)S(1)}, f32[6,4,6,1]{3,2,1,0:T(8,128)S(1)}, u32[]{:S(2)}, u32[]{:S(2)}) collective-permute-start(f32[6,4,6,1]{3,2,1,0:T(8,128)S(1)} %get-tuple-element.234), channel_id=1, source_target_pairs={{0,1},{1,2},{2,3},{3,4},{4,5},{5,6},{6,7},{7,8},{8,9},{9,10},{10,1... | collective-permute-start | bytes 1736 | tf_op jit(solution)/shard_map/ppermute | solution.py:19
  28.6 8.5 %collective-permute-start.5 = (f32[3,4,1,128]{3,2,1,0:T(1,128)S(1)}, f32[3,4,1,128]{3,2,1,0:T(1,128)S(1)}, u32[]{:S(2)}, u32[]{:S(2)}) collective-permute-start(f32[3,4,1,128]{3,2,1,0:T(1,128)S(1)} %get-tuple-element.289), channel_id=1, source_target_pairs={{64,0},{128,64},{192,128},{256,192},{320,256},{384,320},{448,384},... | collective-permute-start | bytes 18440 | tf_op jit(solution)/shard_map/ppermute | solution.py:20
  30.5 7.3 %collective-permute-start.4 = (f32[3,4,1,128]{3,2,1,0:T(1,128)S(1)}, f32[3,4,1,128]{3,2,1,0:T(1,128)S(1)}, u32[]{:S(2)}, u32[]{:S(2)}) collective-permute-start(f32[3,4,1,128]{3,2,1,0:T(1,128)S(1)} %get-tuple-element.288), channel_id=1, source_target_pairs={{0,64},{64,128},{128,192},{192,256},{256,320},{320,384},{384,448},... | collective-permute-start | bytes 18440 | tf_op jit(solution)/shard_map/ppermute | solution.py:19
  37.9 5.7 collective-permute-start.7
  39.8 8.2 %collective-permute-start.6 = (f32[3,4,6,1]{3,2,1,0:T(8,128)S(1)}, f32[3,4,6,1]{3,2,1,0:T(8,128)S(1)}, u32[]{:S(2)}, u32[]{:S(2)}) collective-permute-start(f32[3,4,6,1]{3,2,1,0:T(8,128)S(1)} %get-tuple-element.256), channel_id=1, source_target_pairs={{0,1},{1,2},{2,3},{3,4},{4,5},{5,6},{6,7},{7,8},{8,9},{9,10},{10,1... | collective-permute-start | bytes 872 | tf_op jit(solution)/shard_map/ppermute | solution.py:19
  43.6 15.2 %copy-start = (s32[2048,1]{0,1:T(1,128)S(1)}, s32[2048,1]{0,1:T(1,128)}, u32[]{:S(2)}) copy-start(s32[2048,1]{0,1:T(1,128)} %param.21) | copy-start | bytes 24580
  51.1 12.7 %collective-permute-start.9 = (f32[6,4,1,128]{3,2,1,0:T(1,128)S(1)}, f32[6,4,1,128]{3,2,1,0:T(1,128)S(1)}, u32[]{:S(2)}, u32[]{:S(2)}) collective-permute-start(f32[6,4,1,128]{3,2,1,0:T(1,128)S(1)} %get-tuple-element.255), channel_id=1, source_target_pairs={{64,0},{128,64},{192,128},{256,192},{320,256},{384,320},{448,384},... | collective-permute-start | bytes 36872 | tf_op jit(solution)/shard_map/ppermute | solution.py:20
  53.1 10.8 %collective-permute-start.8 = (f32[6,4,1,128]{3,2,1,0:T(1,128)S(1)}, f32[6,4,1,128]{3,2,1,0:T(1,128)S(1)}, u32[]{:S(2)}, u32[]{:S(2)}) collective-permute-start(f32[6,4,1,128]{3,2,1,0:T(1,128)S(1)} %get-tuple-element.254), channel_id=1, source_target_pairs={{0,64},{64,128},{128,192},{192,256},{256,320},{320,384},{384,448},... | collective-permute-start | bytes 36872 | tf_op jit(solution)/shard_map/ppermute | solution.py:19
  64.0 17.1 %collective-permute-start.11 = (f32[6,4,6,1]{3,2,1,0:T(8,128)S(1)}, f32[6,4,6,1]{3,2,1,0:T(8,128)S(1)}, u32[]{:S(2)}, u32[]{:S(2)}) collective-permute-start(f32[6,4,6,1]{3,2,1,0:T(8,128)S(1)} %get-tuple-element.230), channel_id=1, source_target_pairs={{1,0},{2,1},{3,2},{4,3},{5,4},{6,5},{7,6},{8,7},{9,8},{10,9},{11,1... | collective-permute-start | bytes 1736 | tf_op jit(solution)/shard_map/ppermute | solution.py:20
  65.9 15.2 %collective-permute-start.10 = (f32[6,4,6,1]{3,2,1,0:T(8,128)S(1)}, f32[6,4,6,1]{3,2,1,0:T(8,128)S(1)}, u32[]{:S(2)}, u32[]{:S(2)}) collective-permute-start(f32[6,4,6,1]{3,2,1,0:T(8,128)S(1)} %get-tuple-element.229), channel_id=1, source_target_pairs={{0,1},{1,2},{2,3},{3,4},{4,5},{5,6},{6,7},{7,8},{8,9},{9,10},{10,1... | collective-permute-start | bytes 1736 | tf_op jit(solution)/shard_map/ppermute | solution.py:19
  81.8 148.0 %collective-permute-start.13 = (f32[3,4,1,128]{3,2,1,0:T(1,128)S(1)}, f32[3,4,1,128]{3,2,1,0:T(1,128)S(1)}, u32[]{:S(2)}, u32[]{:S(2)}) collective-permute-start(f32[3,4,1,128]{3,2,1,0:T(1,128)S(1)} %get-tuple-element.287), channel_id=1, source_target_pairs={{64,0},{128,64},{192,128},{256,192},{320,256},{384,320},{448,384},... | collective-permute-start | bytes 18440 | tf_op jit(solution)/shard_map/ppermute | solution.py:20
  83.7 146.1 %collective-permute-start.12 = (f32[3,4,1,128]{3,2,1,0:T(1,128)S(1)}, f32[3,4,1,128]{3,2,1,0:T(1,128)S(1)}, u32[]{:S(2)}, u32[]{:S(2)}) collective-permute-start(f32[3,4,1,128]{3,2,1,0:T(1,128)S(1)} %get-tuple-element.286), channel_id=1, source_target_pairs={{0,64},{64,128},{128,192},{192,256},{256,320},{320,384},{384,448},... | collective-permute-start | bytes 18440 | tf_op jit(solution)/shard_map/ppermute | solution.py:19
  229.9 15.6 %collective-permute-start.15 = (f32[3,4,6,1]{3,2,1,0:T(8,128)S(1)}, f32[3,4,6,1]{3,2,1,0:T(8,128)S(1)}, u32[]{:S(2)}, u32[]{:S(2)}) collective-permute-start(f32[3,4,6,1]{3,2,1,0:T(8,128)S(1)} %get-tuple-element.253), channel_id=1, source_target_pairs={{1,0},{2,1},{3,2},{4,3},{5,4},{6,5},{7,6},{8,7},{9,8},{10,9},{11,1... | collective-permute-start | bytes 872 | tf_op jit(solution)/shard_map/ppermute | solution.py:20
  235.2 10.3 %collective-permute-start.14 = (f32[3,4,6,1]{3,2,1,0:T(8,128)S(1)}, f32[3,4,6,1]{3,2,1,0:T(8,128)S(1)}, u32[]{:S(2)}, u32[]{:S(2)}) collective-permute-start(f32[3,4,6,1]{3,2,1,0:T(8,128)S(1)} %get-tuple-element.252), channel_id=1, source_target_pairs={{0,1},{1,2},{2,3},{3,4},{4,5},{5,6},{6,7},{7,8},{8,9},{9,10},{10,1... | collective-permute-start | bytes 872 | tf_op jit(solution)/shard_map/ppermute | solution.py:19
  245.5 8.8 %copy-start.8 = (s32[2048]{0:T(1024)S(1)}, s32[2048]{0:T(1024)}, u32[]{:S(2)}) copy-start(s32[2048]{0:T(1024)} %param.19) | copy-start | bytes 24580
  245.7 32.8 %copy-start.6 = (f32[3,1024]{1,0:T(4,128)S(1)}, f32[3,1024]{1,0:T(4,128)}, u32[]{:S(2)}) copy-start(f32[3,1024]{1,0:T(4,128)} %param.23) | copy-start | bytes 36868
  248.7 30.1 %collective-permute-start.17 = (f32[6,4,1,128]{3,2,1,0:T(1,128)S(1)}, f32[6,4,1,128]{3,2,1,0:T(1,128)S(1)}, u32[]{:S(2)}, u32[]{:S(2)}) collective-permute-start(f32[6,4,1,128]{3,2,1,0:T(1,128)S(1)} %get-tuple-element.251), channel_id=1, source_target_pairs={{64,0},{128,64},{192,128},{256,192},{320,256},{384,320},{448,384},... | collective-permute-start | bytes 36872 | tf_op jit(solution)/shard_map/ppermute | solution.py:20
  250.6 28.2 %collective-permute-start.16 = (f32[6,4,1,128]{3,2,1,0:T(1,128)S(1)}, f32[6,4,1,128]{3,2,1,0:T(1,128)S(1)}, u32[]{:S(2)}, u32[]{:S(2)}) collective-permute-start(f32[6,4,1,128]{3,2,1,0:T(1,128)S(1)} %get-tuple-element.250), channel_id=1, source_target_pairs={{0,64},{64,128},{128,192},{192,256},{256,320},{320,384},{384,448},... | collective-permute-start | bytes 36872 | tf_op jit(solution)/shard_map/ppermute | solution.py:19
  254.8 8.8 %copy-start.9 = (s32[2048]{0:T(1024)}, s32[2048]{0:T(1024)S(1)}, u32[]{:S(2)}) copy-start(s32[2048]{0:T(1024)S(1)} %get-tuple-element.308) | copy-start | bytes 24580
  263.6 30.3 %all-to-all-start = ((s32[16,1,256]{2,1,0:T(1,128)}), s32[16,1,256]{2,1,0:T(1,128)S(1)}, u32[]{:S(2)}, u32[]{:S(2)}) async-start(s32[16,1,256]{2,1,0:T(1,128)} %bitcast.1), calls=%async_computation | async-start | bytes 32768 | tf_op jit(solution)/shard_map/all_to_all | solution.py:158
  278.9 26.1 %collective-permute-start.19 = (f32[6,4,6,1]{3,2,1,0:T(8,128)S(1)}, f32[6,4,6,1]{3,2,1,0:T(8,128)S(1)}, u32[]{:S(2)}, u32[]{:S(2)}) collective-permute-start(f32[6,4,6,1]{3,2,1,0:T(8,128)S(1)} %get-tuple-element.225), channel_id=1, source_target_pairs={{1,0},{2,1},{3,2},{4,3},{5,4},{6,5},{7,6},{8,7},{9,8},{10,9},{11,1... | collective-permute-start | bytes 1736 | tf_op jit(solution)/shard_map/ppermute | solution.py:20
  285.6 19.4 %collective-permute-start.18 = (f32[6,4,6,1]{3,2,1,0:T(8,128)S(1)}, f32[6,4,6,1]{3,2,1,0:T(8,128)S(1)}, u32[]{:S(2)}, u32[]{:S(2)}) collective-permute-start(f32[6,4,6,1]{3,2,1,0:T(8,128)S(1)} %get-tuple-element.224), channel_id=1, source_target_pairs={{0,1},{1,2},{2,3},{3,4},{4,5},{5,6},{6,7},{7,8},{8,9},{9,10},{10,1... | collective-permute-start | bytes 1736 | tf_op jit(solution)/shard_map/ppermute | solution.py:19
  294.7 48.0 %all-to-all-start.1 = ((s32[16,64,4]{0,2,1:T(4,128)}), s32[16,64,4]{0,2,1:T(4,128)S(1)}, u32[]{:S(2)}, u32[]{:S(2)}) async-start(s32[16,64,4]{0,2,1:T(4,128)} %bitcast.2), calls=%async_computation.1 | async-start | bytes 262144 | tf_op jit(solution)/shard_map/all_to_all | solution.py:157
  305.7 6.7 %collective-permute-start.21 = (f32[3,4,1,128]{3,2,1,0:T(1,128)S(1)}, f32[3,4,1,128]{3,2,1,0:T(1,128)S(1)}, u32[]{:S(2)}, u32[]{:S(2)}) collective-permute-start(f32[3,4,1,128]{3,2,1,0:T(1,128)S(1)} %get-tuple-element.285), channel_id=1, source_target_pairs={{64,0},{128,64},{192,128},{256,192},{320,256},{384,320},{448,384},... | collective-permute-start | bytes 18440 | tf_op jit(solution)/shard_map/ppermute | solution.py:20
  308.8 4.2 collective-permute-start.20
  313.1 12.5 %collective-permute-start.23 = (f32[3,4,6,1]{3,2,1,0:T(8,128)S(1)}, f32[3,4,6,1]{3,2,1,0:T(8,128)S(1)}, u32[]{:S(2)}, u32[]{:S(2)}) collective-permute-start(f32[3,4,6,1]{3,2,1,0:T(8,128)S(1)} %get-tuple-element.249), channel_id=1, source_target_pairs={{1,0},{2,1},{3,2},{4,3},{5,4},{6,5},{7,6},{8,7},{9,8},{10,9},{11,1... | collective-permute-start | bytes 872 | tf_op jit(solution)/shard_map/ppermute | solution.py:20
  317.4 8.5 %collective-permute-start.22 = (f32[3,4,6,1]{3,2,1,0:T(8,128)S(1)}, f32[3,4,6,1]{3,2,1,0:T(8,128)S(1)}, u32[]{:S(2)}, u32[]{:S(2)}) collective-permute-start(f32[3,4,6,1]{3,2,1,0:T(8,128)S(1)} %get-tuple-element.248), channel_id=1, source_target_pairs={{0,1},{1,2},{2,3},{3,4},{4,5},{5,6},{6,7},{7,8},{8,9},{9,10},{10,1... | collective-permute-start | bytes 872 | tf_op jit(solution)/shard_map/ppermute | solution.py:19
  319.8 12.9 %copy-start.5 = (f32[2,2048]{1,0:T(2,128)S(1)}, f32[2,2048]{1,0:T(2,128)}, u32[]{:S(2)}) copy-start(f32[2,2048]{1,0:T(2,128)} %param.20) | copy-start | bytes 49156
  342.7 17.7 %all-to-all-start.2 = ((f32[16,1,768]{2,1,0:T(1,128)}), f32[16,1,768]{2,1,0:T(1,128)S(1)}, u32[]{:S(2)}, u32[]{:S(2)}) async-start(f32[16,1,768]{2,1,0:T(1,128)} %all_to_all.48), calls=%async_computation.2 | async-start | bytes 98304 | tf_op jit(solution)/shard_map/all_to_all | solution.py:194
  362.4 17.3 %all-to-all-start.3 = ((f32[64,1,192]{2,1,0:T(1,128)}), f32[64,1,192]{2,1,0:T(1,128)S(1)}, u32[]{:S(2)}, u32[]{:S(2)}) async-start(f32[64,1,192]{2,1,0:T(1,128)} %reshape.435), calls=%async_computation.3 | async-start | bytes 131072 | tf_op jit(solution)/shard_map/all_to_all | solution.py:193
  404.7 24.8 %copy-start.1 = (f32[3,1024]{0,1:T(8,128)}, f32[3,1024]{0,1:T(8,128)S(1)}, u32[]{:S(2)}) copy-start(f32[3,1024]{0,1:T(8,128)S(1)} %sub.387) | copy-start | bytes 36868
  466.5 5.6 collective-permute-start.25
  469.8 3.2 collective-permute-start.24
  473.1 6.4 %collective-permute-start.27 = (f32[6,4,6,1]{3,2,1,0:T(8,128)S(1)}, f32[6,4,6,1]{3,2,1,0:T(8,128)S(1)}, u32[]{:S(2)}, u32[]{:S(2)}) collective-permute-start(f32[6,4,6,1]{3,2,1,0:T(8,128)S(1)} %get-tuple-element.220), channel_id=1, source_target_pairs={{1,0},{2,1},{3,2},{4,3},{5,4},{6,5},{7,6},{8,7},{9,8},{10,9},{11,1... | collective-permute-start | bytes 1736 | tf_op jit(solution)/shard_map/ppermute | solution.py:20
  477.4 9.2 %collective-permute-start.26 = (f32[6,4,6,1]{3,2,1,0:T(8,128)S(1)}, f32[6,4,6,1]{3,2,1,0:T(8,128)S(1)}, u32[]{:S(2)}, u32[]{:S(2)}) collective-permute-start(f32[6,4,6,1]{3,2,1,0:T(8,128)S(1)} %get-tuple-element.219), channel_id=1, source_target_pairs={{0,1},{1,2},{2,3},{3,4},{4,5},{5,6},{6,7},{7,8},{8,9},{9,10},{10,1... | collective-permute-start | bytes 1736 | tf_op jit(solution)/shard_map/ppermute | solution.py:19
  487.2 7.1 %collective-permute-start.29 = (f32[3,4,1,128]{3,2,1,0:T(1,128)S(1)}, f32[3,4,1,128]{3,2,1,0:T(1,128)S(1)}, u32[]{:S(2)}, u32[]{:S(2)}) collective-permute-start(f32[3,4,1,128]{3,2,1,0:T(1,128)S(1)} %get-tuple-element.283), channel_id=1, source_target_pairs={{64,0},{128,64},{192,128},{256,192},{320,256},{384,320},{448,384},... | collective-permute-start | bytes 18440 | tf_op jit(solution)/shard_map/ppermute | solution.py:20
  490.4 4.6 collective-permute-start.28
  495.1 18.2 %collective-permute-start.31 = (f32[3,4,6,1]{3,2,1,0:T(8,128)S(1)}, f32[3,4,6,1]{3,2,1,0:T(8,128)S(1)}, u32[]{:S(2)}, u32[]{:S(2)}) collective-permute-start(f32[3,4,6,1]{3,2,1,0:T(8,128)S(1)} %get-tuple-element.247), channel_id=1, source_target_pairs={{1,0},{2,1},{3,2},{4,3},{5,4},{6,5},{7,6},{8,7},{9,8},{10,9},{11,1... | collective-permute-start | bytes 872 | tf_op jit(solution)/shard_map/ppermute | solution.py:20
  497.0 16.2 %collective-permute-start.30 = (f32[3,4,6,1]{3,2,1,0:T(8,128)S(1)}, f32[3,4,6,1]{3,2,1,0:T(8,128)S(1)}, u32[]{:S(2)}, u32[]{:S(2)}) collective-permute-start(f32[3,4,6,1]{3,2,1,0:T(8,128)S(1)} %get-tuple-element.246), channel_id=1, source_target_pairs={{0,1},{1,2},{2,3},{3,4},{4,5},{5,6},{6,7},{7,8},{8,9},{9,10},{10,1... | collective-permute-start | bytes 872 | tf_op jit(solution)/shard_map/ppermute | solution.py:19
  512.8 31.3 %copy-start.2 = (f32[3,1024]{0,1:T(8,128)S(1)}, f32[3,1024]{0,1:T(8,128)}, u32[]{:S(2)}) copy-start(f32[3,1024]{0,1:T(8,128)} %copy-done.1) | copy-start | bytes 36868
  514.5 6.9 %collective-permute-start.33 = (f32[6,4,1,128]{3,2,1,0:T(1,128)S(1)}, f32[6,4,1,128]{3,2,1,0:T(1,128)S(1)}, u32[]{:S(2)}, u32[]{:S(2)}) collective-permute-start(f32[6,4,1,128]{3,2,1,0:T(1,128)S(1)} %get-tuple-element.245), channel_id=1, source_target_pairs={{64,0},{128,64},{192,128},{256,192},{320,256},{384,320},{448,384},... | collective-permute-start | bytes 36872 | tf_op jit(solution)/shard_map/ppermute | solution.py:20
  516.4 5.6 collective-permute-start.32
  522.1 7.1 %collective-permute-start.35 = (f32[6,4,6,1]{3,2,1,0:T(8,128)S(1)}, f32[6,4,6,1]{3,2,1,0:T(8,128)S(1)}, u32[]{:S(2)}, u32[]{:S(2)}) collective-permute-start(f32[6,4,6,1]{3,2,1,0:T(8,128)S(1)} %get-tuple-element.215), channel_id=1, source_target_pairs={{1,0},{2,1},{3,2},{4,3},{5,4},{6,5},{7,6},{8,7},{9,8},{10,9},{11,1... | collective-permute-start | bytes 1736 | tf_op jit(solution)/shard_map/ppermute | solution.py:20
  527.1 8.7 %collective-permute-start.34 = (f32[6,4,6,1]{3,2,1,0:T(8,128)S(1)}, f32[6,4,6,1]{3,2,1,0:T(8,128)S(1)}, u32[]{:S(2)}, u32[]{:S(2)}) collective-permute-start(f32[6,4,6,1]{3,2,1,0:T(8,128)S(1)} %get-tuple-element.214), channel_id=1, source_target_pairs={{0,1},{1,2},{2,3},{3,4},{4,5},{5,6},{6,7},{7,8},{8,9},{9,10},{10,1... | collective-permute-start | bytes 1736 | tf_op jit(solution)/shard_map/ppermute | solution.py:19
  536.4 8.5 %collective-permute-start.37 = (f32[3,4,1,128]{3,2,1,0:T(1,128)S(1)}, f32[3,4,1,128]{3,2,1,0:T(1,128)S(1)}, u32[]{:S(2)}, u32[]{:S(2)}) collective-permute-start(f32[3,4,1,128]{3,2,1,0:T(1,128)S(1)} %get-tuple-element.281), channel_id=1, source_target_pairs={{64,0},{128,64},{192,128},{256,192},{320,256},{384,320},{448,384},... | collective-permute-start | bytes 18440 | tf_op jit(solution)/shard_map/ppermute | solution.py:20
  538.4 6.5 %collective-permute-start.36 = (f32[3,4,1,128]{3,2,1,0:T(1,128)S(1)}, f32[3,4,1,128]{3,2,1,0:T(1,128)S(1)}, u32[]{:S(2)}, u32[]{:S(2)}) collective-permute-start(f32[3,4,1,128]{3,2,1,0:T(1,128)S(1)} %get-tuple-element.280), channel_id=1, source_target_pairs={{0,64},{64,128},{128,192},{192,256},{256,320},{320,384},{384,448},... | collective-permute-start | bytes 18440 | tf_op jit(solution)/shard_map/ppermute | solution.py:19
  545.0 17.9 %collective-permute-start.39 = (f32[3,4,6,1]{3,2,1,0:T(8,128)S(1)}, f32[3,4,6,1]{3,2,1,0:T(8,128)S(1)}, u32[]{:S(2)}, u32[]{:S(2)}) collective-permute-start(f32[3,4,6,1]{3,2,1,0:T(8,128)S(1)} %get-tuple-element.243), channel_id=1, source_target_pairs={{1,0},{2,1},{3,2},{4,3},{5,4},{6,5},{7,6},{8,7},{9,8},{10,9},{11,1... | collective-permute-start | bytes 872 | tf_op jit(solution)/shard_map/ppermute | solution.py:20
  546.9 16.0 %collective-permute-start.38 = (f32[3,4,6,1]{3,2,1,0:T(8,128)S(1)}, f32[3,4,6,1]{3,2,1,0:T(8,128)S(1)}, u32[]{:S(2)}, u32[]{:S(2)}) collective-permute-start(f32[3,4,6,1]{3,2,1,0:T(8,128)S(1)} %get-tuple-element.242), channel_id=1, source_target_pairs={{0,1},{1,2},{2,3},{3,4},{4,5},{5,6},{6,7},{7,8},{8,9},{9,10},{10,1... | collective-permute-start | bytes 872 | tf_op jit(solution)/shard_map/ppermute | solution.py:19
  564.2 6.7 %collective-permute-start.41 = (f32[6,4,1,128]{3,2,1,0:T(1,128)S(1)}, f32[6,4,1,128]{3,2,1,0:T(1,128)S(1)}, u32[]{:S(2)}, u32[]{:S(2)}) collective-permute-start(f32[6,4,1,128]{3,2,1,0:T(1,128)S(1)} %get-tuple-element.241), channel_id=1, source_target_pairs={{64,0},{128,64},{192,128},{256,192},{320,256},{384,320},{448,384},... | collective-permute-start | bytes 36872 | tf_op jit(solution)/shard_map/ppermute | solution.py:20
  566.1 5.4 collective-permute-start.40
  571.7 6.9 %collective-permute-start.43 = (f32[6,4,6,1]{3,2,1,0:T(8,128)S(1)}, f32[6,4,6,1]{3,2,1,0:T(8,128)S(1)}, u32[]{:S(2)}, u32[]{:S(2)}) collective-permute-start(f32[6,4,6,1]{3,2,1,0:T(8,128)S(1)} %get-tuple-element.210), channel_id=1, source_target_pairs={{1,0},{2,1},{3,2},{4,3},{5,4},{6,5},{7,6},{8,7},{9,8},{10,9},{11,1... | collective-permute-start | bytes 1736 | tf_op jit(solution)/shard_map/ppermute | solution.py:20
  576.7 8.7 %collective-permute-start.42 = (f32[6,4,6,1]{3,2,1,0:T(8,128)S(1)}, f32[6,4,6,1]{3,2,1,0:T(8,128)S(1)}, u32[]{:S(2)}, u32[]{:S(2)}) collective-permute-start(f32[6,4,6,1]{3,2,1,0:T(8,128)S(1)} %get-tuple-element.209), channel_id=1, source_target_pairs={{0,1},{1,2},{2,3},{3,4},{4,5},{5,6},{6,7},{7,8},{8,9},{9,10},{10,1... | collective-permute-start | bytes 1736 | tf_op jit(solution)/shard_map/ppermute | solution.py:19
  586.0 7.6 %collective-permute-start.45 = (f32[3,4,1,128]{3,2,1,0:T(1,128)S(1)}, f32[3,4,1,128]{3,2,1,0:T(1,128)S(1)}, u32[]{:S(2)}, u32[]{:S(2)}) collective-permute-start(f32[3,4,1,128]{3,2,1,0:T(1,128)S(1)} %get-tuple-element.279), channel_id=1, source_target_pairs={{64,0},{128,64},{192,128},{256,192},{320,256},{384,320},{448,384},... | collective-permute-start | bytes 18440 | tf_op jit(solution)/shard_map/ppermute | solution.py:20
  587.9 6.4 %collective-permute-start.44 = (f32[3,4,1,128]{3,2,1,0:T(1,128)S(1)}, f32[3,4,1,128]{3,2,1,0:T(1,128)S(1)}, u32[]{:S(2)}, u32[]{:S(2)}) collective-permute-start(f32[3,4,1,128]{3,2,1,0:T(1,128)S(1)} %get-tuple-element.278), channel_id=1, source_target_pairs={{0,64},{64,128},{128,192},{192,256},{256,320},{320,384},{384,448},... | collective-permute-start | bytes 18440 | tf_op jit(solution)/shard_map/ppermute | solution.py:19
  594.4 5.3 collective-permute-start.47
  596.3 8.2 %collective-permute-start.46 = (f32[3,4,6,1]{3,2,1,0:T(8,128)S(1)}, f32[3,4,6,1]{3,2,1,0:T(8,128)S(1)}, u32[]{:S(2)}, u32[]{:S(2)}) collective-permute-start(f32[3,4,6,1]{3,2,1,0:T(8,128)S(1)} %get-tuple-element.238), channel_id=1, source_target_pairs={{0,1},{1,2},{2,3},{3,4},{4,5},{5,6},{6,7},{7,8},{8,9},{9,10},{10,1... | collective-permute-start | bytes 872 | tf_op jit(solution)/shard_map/ppermute | solution.py:19
where the time goes:
time: 617 us; the launch traced here: 606 us
  local copies, waits for them, and re-layouts  237 us (38%)
  starting transfers between devices  204 us (33%)
  other arithmetic  79.9 us (13%)
  waiting for transfers between devices  55.8 us (9%)
  blocking collectives  26.6 us (4%)
    gather x12, local copies, waits for them, and re-layouts, shards(): first_pos = jnp.searchsorted(sorted_owner, sorted_owner, side='left')  141 us
    ppermute x24, starting transfers between devices, extended(): before = lax.ppermute(last, axis, up)  84.9 us
    ppermute x24, starting transfers between devices, extended(): after = lax.ppermute(first, axis, down)  73.3 us
    ppermute x24, waiting for transfers between devices, extended(): before = lax.ppermute(last, axis, up)  42.2 us
    scatter-add x3, other arithmetic, shards(): load_map = jnp.zeros((2, depth_len * rows_x * span_local), jnp.float32).a...  35.6 us
    scatter-add x1, other arithmetic, shards(): jnp.zeros((steps_count, channel_count), jnp.float32).at[:, incoming_ids]  22.7 us
    gather x6, local copies, waits for them, and re-layouts, shards(): windows = window_sums(strains[:2], GAUGE).reshape(2, -1)[:, segment_start]  17.4 us
    all_to_all x1, blocking collectives, shards(): lax.all_to_all(lax.all_to_all(reply, 'gx', split_axis=0, concat_axis=0, t...  15.2 us
  transfers between devices with their start and end apart: 52, of which 18 were waited for; matrix products, arithmetic and copies ran while one was open for 39% of the time, Pallas kernels for 0%

commit v1 on v0

v1 whole, which is shorter than its diff:
```python
import functools

import jax
import jax.numpy as jnp
from jax import lax
from jax.experimental import pallas as pl
from jax.experimental.pallas import tpu as pltpu
from jax.sharding import PartitionSpec as P

GAUGE = 8
DT = 0.25
PIECES = 3
STEPS = 3
NF = 14
MESH = pl.DeviceIdType.MESH
NT = (((1,), (1,)), ((), ()))
NN = (((1,), (0,)), ((), ()))


def iota(shape, dim):
    return lax.broadcasted_iota(jnp.int32, shape, dim)


def split(x):
    parts = []
    for _ in range(PIECES):
        part = x.astype(jnp.bfloat16)
        parts.append(part)
        x = x - part.astype(jnp.float32)
    return parts


def dot(a, b, dims):
    return lax.dot_general(a, b, dims, preferred_element_type=jnp.float32)


def dot_split(x, b, dims):
    parts = split(x)
    rows = x.shape[0]
    stacked = dot(jnp.concatenate(parts, axis=0), b, dims)
    total = stacked[:rows]
    for i in range(1, PIECES):
        total = total + stacked[i * rows : (i + 1) * rows]
    return total


def ones_where(mask):
    return jnp.where(mask, 1.0, 0.0).astype(jnp.bfloat16)


def ahead(f, axis):
    return pltpu.roll(f, f.shape[axis] - 1, axis) - f


def behind(f, axis):
    return f - pltpu.roll(f, 1, axis)


def time_step(ext, mats, emit):
    def plane(ref, f, z):
        return ref[f, pl.ds(16 * z, 16), :]

    def ahead_z(f, z):
        return (plane(ext, f, z + 1) if z < 3 else 0.0) - plane(ext, f, z)

    def behind_z(f, z):
        here = plane(ext, f, z)
        return here - plane(ext, f, z - 1) if z > 0 else here

    for z in range(4):
        scale = DT * plane(mats, 0, z)
        sxy, sxz, syz = plane(ext, 6, z), plane(ext, 7, z), plane(ext, 8, z)
        ax = ahead(plane(ext, 3, z), 0) + behind(sxy, 1) + behind_z(7, z)
        ay = behind(sxy, 0) + ahead(plane(ext, 4, z), 1) + behind_z(8, z)
        az = behind(sxz, 0) + behind(syz, 1) + ahead_z(5, z)
        for f, a in enumerate((ax, ay, az)):
            ext[f, pl.ds(16 * z, 16), :] = plane(ext, f, z) + scale * a
    for z in range(4):
        vx, vy, vz = plane(ext, 0, z), plane(ext, 1, z), plane(ext, 2, z)
        exx = behind(vx, 0)
        eyy = behind(vy, 1)
        ezz = behind_z(2, z)
        exy = ahead(vx, 1) + ahead(vy, 0)
        exz = ahead_z(0, z) + ahead(vz, 0)
        eyz = ahead_z(1, z) + ahead(vz, 1)
        emit(z, [e[4:8, 0:128] for e in (exx, eyy, ezz, exy, exz, eyz)])
        lam, mu = plane(mats, 1, z), plane(mats, 2, z)
        dil = lam * (exx + eyy + ezz)
        for f, e in ((3, exx), (4, eyy), (5, ezz)):
            ext[f, pl.ds(16 * z, 16), :] = plane(ext, f, z) + DT * (dil + 2.0 * mu * e)
        for f, e in ((6, exy), (7, exz), (8, eyz)):
            ext[f, pl.ds(16 * z, 16), :] = plane(ext, f, z) + DT * mu * e


def kernel(
    ngx,
    ngy,
    npart,
    state,
    lam,
    mu,
    buoy,
    scell,
    swave,
    start,
    weight,
    owner,
    chan,
    obs,
    res_out,
    grad_out,
    own,
    xr,
    strip,
    yr,
    ext,
    mats,
    srcs,
    es,
    ad,
    glhs,
    colb,
    rank,
    win,
    lane1h,
    obs32,
    sa,
    ra,
    sb,
    rb,
    arr,
    chan1h,
    hirow,
    sb2,
    rb2,
    sa2,
    ra2,
    load,
    xr2,
    strip2,
    yr2,
    halo2,
    exl,
    hsend,
    hrecv,
    h2send,
    h2recv,
    esend,
    erecv,
):
    gx, gy = lax.axis_index("gx"), lax.axis_index("gy")
    nchunk = npart // 128
    gy_bits = ngy.bit_length() - 1
    right_x, left_x = lax.rem(gx + 1, ngx), lax.rem(gx + ngx - 1, ngx)
    right_y, left_y = lax.rem(gy + 1, ngy), lax.rem(gy + ngy - 1, ngy)
    first_x, last_x = gx == 0, gx == ngx - 1
    first_y, last_y = gy == 0, gy == ngy - 1

    if ngx < 16 or ngy < 64:
        ra[...] = jnp.zeros_like(ra)
        rb[...] = jnp.zeros_like(rb)
        rb2[...] = jnp.zeros_like(rb2)
        ra2[...] = jnp.zeros_like(ra2)

    barrier = pltpu.get_barrier_semaphore()

    def greet(x, y):
        pl.semaphore_signal(barrier, inc=1, device_id={"gx": x, "gy": y}, device_id_type=MESH)

    for x in (left_x, right_x):
        for y in (left_y, right_y):
            greet(x, y)

    @pl.loop(1, ngx)
    def _(i):
        greet(lax.rem(gx + i, ngx), gy)

    @pl.loop(1, ngy)
    def _(i):
        greet(gx, lax.rem(gy + i, ngy))

    cell = scell[...]
    nsrc = cell.shape[1]
    key = iota((48, nsrc), 0)
    wave = jnp.concatenate([jnp.broadcast_to(swave[t : t + 1, :], (16, nsrc)) for t in range(STEPS)], axis=0)
    lhs = jnp.where((key & 15) == (cell >> 7), wave, 0.0)
    srcs[...] = dot_split(lhs, ones_where(iota((128, nsrc), 0) == (cell & 127)), NT)
    own[0:144, :] = state[...]
    for f in (3, 4, 5):
        own[16 * f : 16 * f + 16, :] = state[16 * f : 16 * f + 16, :] + srcs[0:16, :]
    own[144:160, :] = buoy[...]
    own[160:176, :] = lam[...]
    own[176:192, :] = mu[...]
    own[192:224, :] = srcs[16:48, :]

    lane = iota((8, 128), 1)
    sub = iota((8, 128), 0)
    low4 = (lane & 7) < 4

    def pack(tile_of, groups, put):
        for u in range(-(-groups // 16)):
            acc = [jnp.zeros((8, 128), jnp.float32)] * 2
            for k in range(min(16, groups - 16 * u)):
                tile = tile_of(16 * u + k)
                here = (lane >> 3) == k
                acc[0] = jnp.where(here, pltpu.roll(tile, (8 * k - 124) % 128, 1), acc[0])
                acc[1] = jnp.where(here, pltpu.roll(tile, (8 * k + 4) % 128, 1), acc[1])
            for side in range(2):
                put(side, u, acc[side])

    def put_strip(side, u, value):
        strip[side, pl.ds(8 * u, 8), :] = value

    pack(lambda i: own[8 * i : 8 * i + 8, :], 2 * NF, put_strip)

    ownf = owner[...].astype(jnp.float32)
    cols = jnp.concatenate([ownf, jnp.zeros((128 - nchunk, 128), jnp.float32)], axis=0).T
    for c in range(nchunk):
        colb[c] = jnp.broadcast_to(cols[:, c : c + 1], (128, 128))
    earlier = iota((128, 128), 0) < iota((128, 128), 1)

    @pl.loop(0, nchunk)
    def _(c):
        row = jnp.broadcast_to(owner[pl.ds(c, 1), :].astype(jnp.float32), (128, 128))
        same = jnp.where((colb[c] == row) & earlier, 1.0, 0.0)

        def more(q, count):
            hit = jnp.where(colb[q] == row, 1.0, 0.0)
            return count + hit.reshape(16, 8, 128).sum(axis=0)

        count = lax.fori_loop(0, c, more, same.reshape(16, 8, 128).sum(axis=0))
        rank[pl.ds(c, 1), :] = jnp.sum(count, axis=0, keepdims=True)

    mats[...] = jnp.zeros_like(mats)
    ext[...] = jnp.zeros_like(ext)
    exl[...] = jnp.zeros_like(exl)
    glhs[...] = jnp.zeros_like(glhs)
    obs32[...] = jnp.zeros_like(obs32)
    for i in range(8):
        obs32[4 * i : 4 * i + 3, :] = obs[:, 128 * i : 128 * i + 128]

    pl.semaphore_wait(barrier, ngx - 1 + ngy - 1 + 4)

    def halo_copies(rows, rows_to, strips, strips_to, send, recv):
        plan = [
            (rows, rows_to.at[0], right_x, gy),
            (rows, rows_to.at[1], left_x, gy),
            (strips.at[0], strips_to.at[1, 0], gx, right_y),
            (strips.at[1], strips_to.at[1, 1], gx, left_y),
            (strips.at[0], strips_to.at[0, 0], right_x, right_y),
            (strips.at[1], strips_to.at[0, 1], right_x, left_y),
            (strips.at[0], strips_to.at[2, 0], left_x, right_y),
            (strips.at[1], strips_to.at[2, 1], left_x, left_y),
        ]
        copies = [
            pltpu.make_async_remote_copy(
                src_ref=src,
                dst_ref=dst,
                send_sem=send.at[i],
                recv_sem=recv.at[i],
                device_id={"gx": x, "gy": y},
                device_id_type=MESH,
            )
            for i, (src, dst, x, y) in enumerate(plan)
        ]
        for copy in copies:
            copy.start()
        return copies

    copies = halo_copies(own, xr, strip, yr, hsend, hrecv)

    def chunk_key(c, width):
        own_c = jnp.concatenate([owner[c + i : c + i + 1, :] for i in range(width)], axis=1)
        rank_c = jnp.concatenate([rank[c + i : c + i + 1, :] for i in range(width)], axis=1).astype(jnp.int32)
        return own_c, rank_c

    def row_of(c, width):
        start_c = jnp.concatenate([start[c + i : c + i + 1, :] for i in range(width)], axis=1)
        row_c = (start_c * 8666) >> 20
        return start_c, row_c

    for c in range(nchunk):
        start_c, row_c = row_of(c, 1)
        ahead_c = iota((128, 128), 0) - (start_c - 121 * row_c)
        win[:, 128 * c : 128 * c + 128] = ones_where((ahead_c >= 0) & (ahead_c < GAUGE))
        own_c, rank_c = chunk_key(c, 1)
        lane_c = (own_c & (ngy - 1)) * 2 + (rank_c & 1)
        lane1h[:, 128 * c : 128 * c + 128] = ones_where(iota((128, 128), 0) == lane_c)

    def place_rows(g, rows_ref, drop):
        for f in range(NF):
            for z in range(4):
                part = rows_ref[16 * f + 4 * z : 16 * f + 4 * z + 4, :]
                if drop is not None:
                    part = jnp.where(drop, 0.0, part)
                put_ext(f, slice(16 * z + 4 * g, 16 * z + 4 * g + 4), slice(0, 128), part)

    def put_ext(f, rows, lanes, value):
        if f < 9:
            ext[f, rows, lanes] = value
        elif f < 12:
            mats[f - 9, rows, lanes] = value
        else:
            exl[f - 12, rows, lanes] = value

    def comb(strips, g, u):
        low = jnp.where(first_y, 0.0, strips[g, 0, pl.ds(8 * u, 8), :])
        high = jnp.where(last_y, 0.0, strips[g, 1, pl.ds(8 * u, 8), :])
        both = jnp.where(low4, low, high)
        if g == 0:
            both = jnp.where(first_x, 0.0, both)
        if g == 2:
            both = jnp.where(last_x, 0.0, both)
        return both

    place_rows(1, own, None)
    for copy in copies:
        copy.wait()
    place_rows(0, xr.at[0], first_x)
    place_rows(2, xr.at[1], last_x)
    for g in range(3):
        for u in range(2):
            both = comb(yr, g, u)
            for k in range(min(16, 2 * NF - 16 * u)):
                f, h = divmod(16 * u + k, 2)
                tile = pltpu.roll(both, (124 - 8 * k) % 128, 1)
                for i in range(2):
                    z = 2 * h + i
                    put_ext(f, slice(16 * z + 4 * g, 16 * z + 4 * g + 4), slice(128, 256), tile[4 * i : 4 * i + 4, :])

    for t in range(STEPS):
        if t > 0:
            for f in (3, 4, 5):
                ext[f] = ext[f] + exl[t - 1]

        def emit(z, e, t=t):
            for i in range(6):
                es[6 * t + i, pl.ds(4 * z, 4), :] = e[i]
            for f in range(2):
                glhs[pl.ds(32 * z + 4 * f + t, 4, stride=8), :] = e[f]

        time_step(ext, mats, emit)

    def sub_of(width):
        return iota((8, width), 0)

    def weights(c, width):
        both = weight[:, 128 * c : 128 * (c + width)]
        return jnp.where(sub_of(128 * width) < 4, both[0:1, :], both[1:2, :])

    width = 2 if nchunk % 2 == 0 else 1
    wide = 128 * width
    gpieces = jnp.concatenate(split(glhs[...]), axis=0)
    acc = jnp.zeros((PIECES * 128, 128), jnp.float32)
    for c in range(0, nchunk, width):
        lanes = slice(128 * c, 128 * c + wide)
        _, row_c = row_of(c, width)
        got = dot(gpieces, win[:, lanes], NN)
        picked = jnp.zeros((8, wide), jnp.float32)
        for r in range(16):
            tile = got[8 * r : 8 * r + 8]
            for i in range(1, PIECES):
                tile = tile + got[128 * i + 8 * r : 128 * i + 8 * r + 8]
            picked = picked + jnp.where(row_c == r, tile, 0.0)
        picked = picked * weights(c, width)
        picked = picked + pltpu.roll(picked, 4, 0)
        chan_c = jnp.concatenate([chan[c + i : c + i + 1, :] for i in range(width)], axis=1)
        picked = jnp.where((sub_of(wide) & 3) == 3, chan_c.astype(jnp.float32), picked)
        own_c, rank_c = chunk_key(c, width)
        key_c = (own_c >> gy_bits) * 2 + (rank_c >> 1)
        hit = (iota((128, wide), 0) >> 2) == key_c
        parts = [
            jnp.where(hit, jnp.concatenate([part.astype(jnp.float32)] * 16, axis=0), 0.0).astype(jnp.bfloat16)
            for part in split(picked)
        ]
        acc = acc + dot(jnp.concatenate(parts, axis=0), lane1h[:, lanes], NT)
    total = acc[0:128]
    for i in range(1, PIECES):
        total = total + acc[128 * i : 128 * i + 128]
    sa[...] = total.reshape(16, 8, 128)

    def exchange(stage, src, dst, count, axis, me):
        unit = src.shape[0] // (16 if axis == "gx" else 64)
        send, recv = esend.at[stage], erecv.at[stage]
        other = "gy" if axis == "gx" else "gx"
        there = gy if axis == "gx" else gx

        def part(ref, i):
            return ref.at[pl.ds(i * unit, unit)]

        mine = pltpu.make_async_copy(part(src, me), part(dst, me), recv)
        mine.start()

        @pl.loop(1, count)
        def _(i):
            to = lax.rem(me + i, count)
            pltpu.make_async_remote_copy(
                src_ref=part(src, to),
                dst_ref=part(dst, me),
                send_sem=send,
                recv_sem=recv,
                device_id={axis: to, other: there},
                device_id_type=MESH,
            ).start()

        whole = dst.at[pl.ds(0, count * unit)]
        pltpu.make_async_copy(whole, whole, recv).wait()
        less = src.at[pl.ds(0, (count - 1) * unit)]
        pltpu.make_async_copy(less, less, send).wait()

    exchange(0, sa, ra, ngx, "gx", gx)
    sb[...] = ra[...].reshape(128, 128).T.reshape(64, 2, 128)
    exchange(1, sb, rb, ngy, "gy", gy)
    arr[...] = rb[...].reshape(128, 128).T

    acc = jnp.zeros((PIECES * 32, 128), jnp.float32)
    sub256 = sub_of(256) >> 2
    for d in range(16):
        tile = arr[8 * d : 8 * d + 8, :]
        turned = pltpu.roll(tile, 4, 0)
        both = jnp.concatenate([jnp.where(sub < 4, tile, turned), jnp.where(sub < 4, turned, tile)], axis=1)
        ids = both[3:4, :].astype(jnp.int32)
        onehot = ones_where(iota((128, 256), 0) == (ids & 127))
        chan1h[:, 256 * d : 256 * d + 256] = onehot
        hi = ids >> 7
        hirow[d : d + 1, :] = hi
        parts = []
        for part in split(both):
            part = part.astype(jnp.float32)
            for j in range(4):
                parts.append(jnp.where(hi == sub256 + 2 * j, part, 0.0).astype(jnp.bfloat16))
        acc = acc + dot(jnp.concatenate(parts, axis=0), onehot, NT)
    sums = acc[0:32]
    for i in range(1, PIECES):
        sums = sums + acc[32 * i : 32 * i + 32]
    sums = jnp.where((iota((32, 128), 0) & 3) == 3, 0.0, sums - obs32[...])
    for i in range(8):
        res_out[:, 128 * i : 128 * i + 128] = sums[4 * i : 4 * i + 3, :]

    pieces = jnp.concatenate(split(sums), axis=0)
    for d in range(16):
        got = dot(pieces, chan1h[:, 256 * d : 256 * d + 256], NN)
        hi = hirow[d : d + 1, :]
        picked = jnp.zeros((8, 256), jnp.float32)
        for j in range(4):
            tile = got[8 * j : 8 * j + 8]
            for i in range(1, PIECES):
                tile = tile + got[32 * i + 8 * j : 32 * i + 8 * j + 8]
            picked = picked + jnp.where(hi == sub256 + 2 * j, tile, 0.0)
        picked = picked + pltpu.roll(picked, 4, 0)
        arr[8 * d : 8 * d + 8, :] = jnp.where(sub < 4, picked[:, 0:128], picked[:, 128:256])
    sb2[...] = arr[...].T.reshape(64, 2, 128)
    exchange(2, sb2, rb2, ngy, "gy", gy)
    sa2[...] = rb2[...].reshape(128, 128).T.reshape(16, 8, 128)
    exchange(3, sa2, ra2, ngx, "gx", gx)

    pieces = jnp.concatenate(split(ra2[...].reshape(128, 128)), axis=0)
    acc = jnp.zeros((PIECES * 128, 128), jnp.float32)
    for c in range(0, nchunk, width):
        lanes = slice(128 * c, 128 * c + wide)
        got = dot(pieces, lane1h[:, lanes], NN)
        own_c, rank_c = chunk_key(c, width)
        key_c = (own_c >> gy_bits) * 2 + (rank_c >> 1)
        half = sub_of(wide) >> 2
        picked = jnp.zeros((8, wide), jnp.float32)
        for r in range(16):
            tile = got[8 * r : 8 * r + 8]
            for i in range(1, PIECES):
                tile = tile + got[128 * i + 8 * r : 128 * i + 8 * r + 8]
            picked = picked + jnp.where(key_c == half + 2 * r, tile, 0.0)
        picked = (picked + pltpu.roll(picked, 4, 0)) * weights(c, width)
        _, row_c = row_of(c, width)
        hit = (iota((128, wide), 0) >> 3) == row_c
        parts = [
            jnp.where(hit, jnp.concatenate([part.astype(jnp.float32)] * 16, axis=0), 0.0).astype(jnp.bfloat16)
            for part in split(picked)
        ]
        acc = acc + dot(jnp.concatenate(parts, axis=0), win[:, lanes], NT)
    total = acc[0:128]
    for i in range(1, PIECES):
        total = total + acc[128 * i : 128 * i + 128]
    load[...] = total

    def put_strip2(side, u, value):
        strip2[side] = value

    pack(lambda i: load[8 * i : 8 * i + 8, :], 16, put_strip2)
    copies = halo_copies(load, xr2, strip2, yr2, h2send, h2recv)
    ext[...] = jnp.zeros_like(ext)
    for copy in copies:
        copy.wait()
    for g in range(3):
        both = comb(yr2, g, 0)
        for k in range(16):
            halo2[g, pl.ds(8 * k, 8), :] = pltpu.roll(both, (124 - 8 * k) % 128, 1)
    sources = ((xr2.at[0], first_x), (load, None), (xr2.at[1], last_x))
    for f in range(2):
        for t in range(STEPS):
            for z in range(4):
                rows = pl.ds(32 * z + 4 * f + t, 4, stride=8)
                for g, (ref, drop) in enumerate(sources):
                    part = ref[rows, :]
                    if drop is not None:
                        part = jnp.where(drop, 0.0, part)
                    exl[2 * t + f, 16 * z + 4 * g : 16 * z + 4 * g + 4, 0:128] = part
                    exl[2 * t + f, 16 * z + 4 * g : 16 * z + 4 * g + 4, 128:256] = halo2[g, rows, :]

    lam_grad = jnp.zeros((16, 128), jnp.float32)
    mu_grad = jnp.zeros((16, 128), jnp.float32)
    for k in range(STEPS):
        t = STEPS - 1 - k
        for f in range(2):
            ext[3 + f] = ext[3 + f] + exl[2 * t + f]

        def emit(z, e):
            for i in range(6):
                ad[i, pl.ds(4 * z, 4), :] = e[i]

        time_step(ext, mats, emit)
        fwd = [es[6 * t + i] for i in range(6)]
        adj = [ad[i] for i in range(6)]
        prod = [a * b for a, b in zip(fwd, adj)]
        lam_grad = lam_grad + (fwd[0] + fwd[1] + fwd[2]) * (adj[0] + adj[1] + adj[2])
        mu_grad = mu_grad + (2.0 * (prod[0] + prod[1] + prod[2]) + prod[3] + prod[4] + prod[5])
    grad_out[0:16, :] = lam_grad
    grad_out[16:32, :] = mu_grad


def shards(
    initial_state,
    lame_lambda,
    shear_modulus,
    buoyancy,
    source_cells,
    source_wavelet,
    segment_start,
    segment_weight,
    partial_owner,
    partial_channel,
    observed_data,
):
    ngx, ngy = lax.axis_size("gx"), lax.axis_size("gy")
    npart = segment_start.shape[0]
    nsrc = source_cells.shape[0]
    f32, bf16 = jnp.float32, jnp.bfloat16
    vmem = pl.BlockSpec(memory_space=pltpu.VMEM)
    dma = pltpu.SemaphoreType.DMA
    scratch = [
        pltpu.VMEM((16 * NF, 128), f32),
        pltpu.VMEM((2, 16 * NF, 128), f32),
        pltpu.VMEM((2, 16, 128), f32),
        pltpu.VMEM((3, 2, 16, 128), f32),
        pltpu.VMEM((9, 64, 256), f32),
        pltpu.VMEM((3, 64, 256), f32),
        pltpu.VMEM((48, 128), f32),
        pltpu.VMEM((6 * STEPS, 16, 128), f32),
        pltpu.VMEM((6, 16, 128), f32),
        pltpu.VMEM((128, 128), f32),
        pltpu.VMEM((npart // 128, 128, 128), f32),
        pltpu.VMEM((npart // 128, 128), f32),
        pltpu.VMEM((128, npart), bf16),
        pltpu.VMEM((128, npart), bf16),
        pltpu.VMEM((32, 128), f32),
        pltpu.VMEM((16, 8, 128), f32),
        pltpu.VMEM((16, 8, 128), f32),
        pltpu.VMEM((64, 2, 128), f32),
        pltpu.VMEM((64, 2, 128), f32),
        pltpu.VMEM((128, 128), f32),
        pltpu.VMEM((128, 4096), bf16),
        pltpu.VMEM((16, 256), jnp.int32),
        pltpu.VMEM((64, 2, 128), f32),
        pltpu.VMEM((64, 2, 128), f32),
        pltpu.VMEM((16, 8, 128), f32),
        pltpu.VMEM((16, 8, 128), f32),
        pltpu.VMEM((128, 128), f32),
        pltpu.VMEM((2, 128, 128), f32),
        pltpu.VMEM((2, 8, 128), f32),
        pltpu.VMEM((3, 2, 8, 128), f32),
        pltpu.VMEM((3, 128, 128), f32),
        pltpu.VMEM((2 * STEPS, 64, 256), f32),
        dma((8,)),
        dma((8,)),
        dma((8,)),
        dma((8,)),
        dma((4,)),
        dma((4,)),
    ]
    residuals, gradients = pl.pallas_call(
        functools.partial(kernel, ngx, ngy, npart),
        out_shape=(
            jax.ShapeDtypeStruct(observed_data.shape, f32),
            jax.ShapeDtypeStruct((32, 128), f32),
        ),
        in_specs=[vmem] * 11,
        out_specs=(vmem, vmem),
        scratch_shapes=scratch,
        compiler_params=pltpu.CompilerParams(collective_id=0, has_side_effects=True),
        name="window",
    )(
        initial_state.reshape(144, 128),
        lame_lambda.reshape(16, 128),
        shear_modulus.reshape(16, 128),
        buoyancy.reshape(16, 128),
        source_cells.reshape(1, nsrc),
        source_wavelet,
        segment_start.reshape(-1, 128),
        segment_weight,
        partial_owner.reshape(-1, 128),
        partial_channel.reshape(-1, 128),
        observed_data,
    )
    return residuals, gradients.reshape(2, 4, 4, 128)


def solution(mesh):
    in_specs = (
        P(None, None, "gx", "gy"),
        P(None, "gx", "gy"),
        P(None, "gx", "gy"),
        P(None, "gx", "gy"),
        P(("gx", "gy")),
        P(None, ("gx", "gy")),
        P(("gx", "gy")),
        P(None, ("gx", "gy")),
        P(("gx", "gy"), None),
        P(("gx", "gy")),
        P(None, ("gx", "gy")),
    )
    out_specs = (P(None, ("gx", "gy")), P(None, None, "gx", "gy"))
    return jax.shard_map(shards, mesh=mesh, in_specs=in_specs, out_specs=out_specs, check_vma=False)
```

time: 617 us -> 70.8 us (0.11)
  the two profiles are of different devices: /device:TPU:9 before, /device:TPU:1 now
where the time goes in v1:
time: 70.8 us; the launch traced here: 70.5 us
  Pallas kernels  67.9 us (96%)
  local copies, waits for them, and re-layouts  1.94 us (3%)
    pallas_call x1, Pallas kernels, shards(): pl.pallas_call(functools.partial(kernel, ngx, ngy, npart), out_shape=(jax...  67.9 us
    unnamed x4, local copies, waits for them, and re-layouts  1.94 us

profile of v1, /device:TPU:1, one launch (start us, length us, event | category | flops | bytes accessed | tf_op | source)
XLA Modules:
  0.0 70.5 jit_solution(3251323502925842550)
XLA Ops:
  0.6 67.9 %window.1 = (f32[3,1024]{1,0:T(4,128)}, f32[32,128]{1,0:T(8,128)}) custom-call(f32[144,128]{1,0:T(8,128)} %bitcast.9, f32[16,128]{1,0:T(8,128)} %bitcast.11, f32[16,128]{1,0:T(8,128)} %bitcast.12, f32[16,128]{1,0:T(8,128)} %bitcast.13, s32[1,64]{1,0:T(1,128)} %bitcast.17, f32[3,64]{1,0:T(4,128)} %swave.1, s32[16,128]{1,0:T(8,128)} %bitcast.14, ...), custom_call_target="tpu_custom_call" | custom-call | tf_op jit(solution)/shard_map/window/pallas_call | solution.py:588
  68.6 0.0 copy-start
  68.6 1.3 %copy.15 = f32[3,1024]{1,0:T(4,128)} copy(f32[3,1024]{1,0:T(4,128)} %get-tuple-element.8) | data formatting | bytes 24576
  69.9 0.0 copy-done
  69.9 0.6 copy.16
Async XLA Ops:
  68.6 1.3 %copy-start = (f32[32,128]{1,0:T(8,128)S(1)}, f32[32,128]{1,0:T(8,128)}, u32[]{:S(2)}) copy-start(f32[32,128]{1,0:T(8,128)} %get-tuple-element.5) | copy-start | bytes 49156

commit v2 on v1

--- a/solution.py
+++ b/solution.py
@@ -96,10 +96,19 @@
     ngx,
     ngy,
     npart,
-    state,
-    lam,
-    mu,
-    buoy,
+    state_in,
+    lam_in,
+    mu_in,
+    buoy_in,
+    scell_in,
+    swave_in,
+    start_in,
+    weight_in,
+    owner_in,
+    chan_in,
+    obs_in,
+    res_out,
+    grad_out,
     scell,
     swave,
     start,
@@ -107,8 +116,8 @@
     owner,
     chan,
     obs,
-    res_out,
-    grad_out,
+    res,
+    grad,
     own,
     xr,
     strip,
@@ -126,13 +135,13 @@
     obs32,
     sa,
     ra,
-    sb,
-    rb,
+    sx,
+    rx,
     arr,
     chan1h,
     hirow,
-    sb2,
-    rb2,
+    sx2,
+    rx2,
     sa2,
     ra2,
     load,
@@ -147,37 +156,75 @@
     h2recv,
     esend,
     erecv,
+    isem,
+    osem,
+    ready,
 ):
     gx, gy = lax.axis_index("gx"), lax.axis_index("gy")
     nchunk = npart // 128
     gy_bits = ngy.bit_length() - 1
+    y_bits = gy_bits // 2
+    ny = 1 << y_bits
+    nx = ngy // ny
     right_x, left_x = lax.rem(gx + 1, ngx), lax.rem(gx + ngx - 1, ngx)
     right_y, left_y = lax.rem(gy + 1, ngy), lax.rem(gy + ngy - 1, ngy)
     first_x, last_x = gx == 0, gx == ngx - 1
     first_y, last_y = gy == 0, gy == ngy - 1
 
     if ngx < 16 or ngy < 64:
-        ra[...] = jnp.zeros_like(ra)
-        rb[...] = jnp.zeros_like(rb)
-        rb2[...] = jnp.zeros_like(rb2)
-        ra2[...] = jnp.zeros_like(ra2)
+        for ref in (ra, rx, rx2, ra2):
+            ref[...] = jnp.zeros_like(ref)
 
     barrier = pltpu.get_barrier_semaphore()
 
     def greet(x, y):
         pl.semaphore_signal(barrier, inc=1, device_id={"gx": x, "gy": y}, device_id_type=MESH)
 
-    for x in (left_x, right_x):
-        for y in (left_y, right_y):
-            greet(x, y)
-
-    @pl.loop(1, ngx)
-    def _(i):
-        greet(lax.rem(gx + i, ngx), gy)
-
-    @pl.loop(1, ngy)
-    def _(i):
-        greet(gx, lax.rem(gy + i, ngy))
+    reads = [
+        pltpu.make_async_copy(src, dst, isem.at[i])
+        for i, (src, dst) in enumerate(
+            (
+                (state_in, own.at[pl.ds(0, 144)]),
+                (scell_in, scell),
+                (swave_in, swave),
+                (buoy_in, own.at[pl.ds(144, 16)]),
+                (lam_in, own.at[pl.ds(160, 16)]),
+                (mu_in, own.at[pl.ds(176, 16)]),
+                (owner_in, owner),
+                (start_in, start),
+                (chan_in, chan),
+                (weight_in, weight),
+                (obs_in, obs),
+            )
+        )
+    ]
+    for read in reads:
+        read.start()
+
+    def far_first(count):
+        return sorted(range(1, count), key=lambda i: -min(i, count - i))
+
+    def peer_z(i):
+        return lax.rem(gx + i, ngx), gy
+
+    def peer_x(i):
+        return gx, lax.rem((gy >> y_bits) + i, nx) * ny + (gy & (ny - 1))
+
+    def peer_y(i):
+        return gx, (gy & ~(ny - 1)) + lax.rem((gy & (ny - 1)) + i, ny)
+
+    greeted = [peer_z(i) for i in far_first(ngx)] + [peer_x(i) for i in far_first(nx)] + [peer_y(i) for i in far_first(ny)]
+    greeted += [(x, y) for y in (left_y, right_y) for x in (gx, left_x, right_x)]
+    for x, y in greeted:
+        greet(x, y)
+
+    mats[...] = jnp.zeros_like(mats)
+    ext[...] = jnp.zeros_like(ext)
+    exl[...] = jnp.zeros_like(exl)
+    glhs[...] = jnp.zeros_like(glhs)
+    obs32[...] = jnp.zeros_like(obs32)
+    for read in reads[:6]:
+        read.wait()
 
     cell = scell[...]
     nsrc = cell.shape[1]
@@ -185,12 +232,8 @@
     wave = jnp.concatenate([jnp.broadcast_to(swave[t : t + 1, :], (16, nsrc)) for t in range(STEPS)], axis=0)
     lhs = jnp.where((key & 15) == (cell >> 7), wave, 0.0)
     srcs[...] = dot_split(lhs, ones_where(iota((128, nsrc), 0) == (cell & 127)), NT)
-    own[0:144, :] = state[...]
     for f in (3, 4, 5):
-        own[16 * f : 16 * f + 16, :] = state[16 * f : 16 * f + 16, :] + srcs[0:16, :]
-    own[144:160, :] = buoy[...]
-    own[160:176, :] = lam[...]
-    own[176:192, :] = mu[...]
+        own[16 * f : 16 * f + 16, :] = own[16 * f : 16 * f + 16, :] + srcs[0:16, :]
     own[192:224, :] = srcs[16:48, :]
 
     lane = iota((8, 128), 1)
@@ -213,33 +256,10 @@
 
     pack(lambda i: own[8 * i : 8 * i + 8, :], 2 * NF, put_strip)
 
-    ownf = owner[...].astype(jnp.float32)
-    cols = jnp.concatenate([ownf, jnp.zeros((128 - nchunk, 128), jnp.float32)], axis=0).T
-    for c in range(nchunk):
-        colb[c] = jnp.broadcast_to(cols[:, c : c + 1], (128, 128))
-    earlier = iota((128, 128), 0) < iota((128, 128), 1)
-
-    @pl.loop(0, nchunk)
-    def _(c):
-        row = jnp.broadcast_to(owner[pl.ds(c, 1), :].astype(jnp.float32), (128, 128))
-        same = jnp.where((colb[c] == row) & earlier, 1.0, 0.0)
-
-        def more(q, count):
-            hit = jnp.where(colb[q] == row, 1.0, 0.0)
-            return count + hit.reshape(16, 8, 128).sum(axis=0)
-
-        count = lax.fori_loop(0, c, more, same.reshape(16, 8, 128).sum(axis=0))
-        rank[pl.ds(c, 1), :] = jnp.sum(count, axis=0, keepdims=True)
-
-    mats[...] = jnp.zeros_like(mats)
-    ext[...] = jnp.zeros_like(ext)
-    exl[...] = jnp.zeros_like(exl)
-    glhs[...] = jnp.zeros_like(glhs)
-    obs32[...] = jnp.zeros_like(obs32)
-    for i in range(8):
-        obs32[4 * i : 4 * i + 3, :] = obs[:, 128 * i : 128 * i + 128]
-
-    pl.semaphore_wait(barrier, ngx - 1 + ngy - 1 + 4)
+    pl.semaphore_wait(barrier, len(greeted))
+    for i in far_first(nx):
+        x, y = peer_x(i)
+        pl.semaphore_signal(ready, inc=1, device_id={"gx": x, "gy": y}, device_id_type=MESH)
 
     def halo_copies(rows, rows_to, strips, strips_to, send, recv):
         plan = [
@@ -268,6 +288,30 @@
         return copies
 
     copies = halo_copies(own, xr, strip, yr, hsend, hrecv)
+    for read in reads[6:]:
+        read.wait()
+
+    ownf = owner[...].astype(jnp.float32)
+    cols = jnp.concatenate([ownf, jnp.zeros((128 - nchunk, 128), jnp.float32)], axis=0).T
+    for c in range(nchunk):
+        colb[c] = jnp.broadcast_to(cols[:, c : c + 1], (128, 128))
+    earlier = iota((128, 128), 0) < iota((128, 128), 1)
+
+    @pl.loop(0, nchunk)
+    def _(c):
+        row = jnp.broadcast_to(owner[pl.ds(c, 1), :].astype(jnp.float32), (128, 128))
+        same = jnp.where((colb[c] == row) & earlier, 1.0, 0.0)
+
+        def more(q, count):
+            hit = jnp.where(colb[q] == row, 1.0, 0.0)
+            return count + hit.reshape(16, 8, 128).sum(axis=0)
+
+        count = lax.fori_loop(0, c, more, same.reshape(16, 8, 128).sum(axis=0))
+        rank[pl.ds(c, 1), :] = jnp.sum(count, axis=0, keepdims=True)
+
+    for i in range(8):
+        obs32[4 * i : 4 * i + 3, :] = obs[:, 128 * i : 128 * i + 128]
+
 
     def chunk_key(c, width):
         own_c = jnp.concatenate([owner[c + i : c + i + 1, :] for i in range(width)], axis=1)
@@ -379,39 +423,34 @@
         total = total + acc[128 * i : 128 * i + 128]
     sa[...] = total.reshape(16, 8, 128)
 
-    def exchange(stage, src, dst, count, axis, me):
-        unit = src.shape[0] // (16 if axis == "gx" else 64)
+    def exchange(stage, peers, me, src, dst):
         send, recv = esend.at[stage], erecv.at[stage]
-        other = "gy" if axis == "gx" else "gx"
-        there = gy if axis == "gx" else gx
-
-        def part(ref, i):
-            return ref.at[pl.ds(i * unit, unit)]
-
-        mine = pltpu.make_async_copy(part(src, me), part(dst, me), recv)
-        mine.start()
-
-        @pl.loop(1, count)
-        def _(i):
-            to = lax.rem(me + i, count)
+        for place, x, y in peers:
             pltpu.make_async_remote_copy(
-                src_ref=part(src, to),
-                dst_ref=part(dst, me),
+                src_ref=src.at[place],
+                dst_ref=dst.at[me],
                 send_sem=send,
                 recv_sem=recv,
-                device_id={axis: to, other: there},
+                device_id={"gx": x, "gy": y},
                 device_id_type=MESH,
             ).start()
-
-        whole = dst.at[pl.ds(0, count * unit)]
+        pltpu.make_async_copy(src.at[me], dst.at[me], recv).start()
+        whole, less = dst.at[pl.ds(0, len(peers) + 1)], src.at[pl.ds(0, len(peers))]
         pltpu.make_async_copy(whole, whole, recv).wait()
-        less = src.at[pl.ds(0, (count - 1) * unit)]
         pltpu.make_async_copy(less, less, send).wait()
 
-    exchange(0, sa, ra, ngx, "gx", gx)
-    sb[...] = ra[...].reshape(128, 128).T.reshape(64, 2, 128)
-    exchange(1, sb, rb, ngy, "gy", gy)
-    arr[...] = rb[...].reshape(128, 128).T
+    z_peers = [(lax.rem(gx + i, ngx), lax.rem(gx + i, ngx), gy) for i in far_first(ngx)]
+    xs = [lax.rem((gy >> y_bits) + i, nx) * ny for i in range(nx)]
+    ys = [lax.rem((gy & (ny - 1)) + i, ny) for i in range(ny)]
+    offsets = [(i, j) for i in range(nx) for j in range(ny) if i or j]
+    offsets.sort(key=lambda o: -min(o[0], nx - o[0]) - min(o[1], ny - o[1]))
+    xy_peers = [(xs[i] + ys[j], gx, xs[i] + ys[j]) for i, j in offsets]
+
+    exchange(0, z_peers, gx, sa, ra)
+    sx[...] = ra[...].reshape(128, 128).T.reshape(64, 2, 128)
+    pl.semaphore_wait(ready, nx - 1)
+    exchange(1, xy_peers, gy, sx, rx)
+    arr[...] = rx[...].reshape(128, 128).T
 
     acc = jnp.zeros((PIECES * 32, 128), jnp.float32)
     sub256 = sub_of(256) >> 2
@@ -435,7 +474,9 @@
         sums = sums + acc[32 * i : 32 * i + 32]
     sums = jnp.where((iota((32, 128), 0) & 3) == 3, 0.0, sums - obs32[...])
     for i in range(8):
-        res_out[:, 128 * i : 128 * i + 128] = sums[4 * i : 4 * i + 3, :]
+        res[:, 128 * i : 128 * i + 128] = sums[4 * i : 4 * i + 3, :]
+    put_res = pltpu.make_async_copy(res, res_out, osem.at[0])
+    put_res.start()
 
     pieces = jnp.concatenate(split(sums), axis=0)
     for d in range(16):
@@ -449,10 +490,10 @@
             picked = picked + jnp.where(hi == sub256 + 2 * j, tile, 0.0)
         picked = picked + pltpu.roll(picked, 4, 0)
         arr[8 * d : 8 * d + 8, :] = jnp.where(sub < 4, picked[:, 0:128], picked[:, 128:256])
-    sb2[...] = arr[...].T.reshape(64, 2, 128)
-    exchange(2, sb2, rb2, ngy, "gy", gy)
-    sa2[...] = rb2[...].reshape(128, 128).T.reshape(16, 8, 128)
-    exchange(3, sa2, ra2, ngx, "gx", gx)
+    sx2[...] = arr[...].T.reshape(64, 2, 128)
+    exchange(2, xy_peers, gy, sx2, rx2)
+    sa2[...] = rx2[...].reshape(128, 128).T.reshape(16, 8, 128)
+    exchange(3, z_peers, gx, sa2, ra2)
 
     pieces = jnp.concatenate(split(ra2[...].reshape(128, 128)), axis=0)
     acc = jnp.zeros((PIECES * 128, 128), jnp.float32)
@@ -522,8 +563,12 @@
         prod = [a * b for a, b in zip(fwd, adj)]
         lam_grad = lam_grad + (fwd[0] + fwd[1] + fwd[2]) * (adj[0] + adj[1] + adj[2])
         mu_grad = mu_grad + (2.0 * (prod[0] + prod[1] + prod[2]) + prod[3] + prod[4] + prod[5])
-    grad_out[0:16, :] = lam_grad
-    grad_out[16:32, :] = mu_grad
+    grad[0:16, :] = lam_grad
+    grad[16:32, :] = mu_grad
+    put_grad = pltpu.make_async_copy(grad, grad_out, osem.at[1])
+    put_grad.start()
+    put_res.wait()
+    put_grad.wait()
 
 
 def shards(
@@ -543,9 +588,18 @@
     npart = segment_start.shape[0]
     nsrc = source_cells.shape[0]
     f32, bf16 = jnp.float32, jnp.bfloat16
-    vmem = pl.BlockSpec(memory_space=pltpu.VMEM)
+    anywhere = pl.BlockSpec(memory_space=pl.ANY)
     dma = pltpu.SemaphoreType.DMA
     scratch = [
+        pltpu.VMEM((1, nsrc), jnp.int32),
+        pltpu.VMEM((STEPS, nsrc), f32),
+        pltpu.VMEM((npart // 128, 128), jnp.int32),
+        pltpu.VMEM((2, npart), f32),
+        pltpu.VMEM((npart // 128, 128), jnp.int32),
+        pltpu.VMEM((npart // 128, 128), jnp.int32),
+        pltpu.VMEM(observed_data.shape, f32),
+        pltpu.VMEM(observed_data.shape, f32),
+        pltpu.VMEM((32, 128), f32),
         pltpu.VMEM((16 * NF, 128), f32),
         pltpu.VMEM((2, 16 * NF, 128), f32),
         pltpu.VMEM((2, 16, 128), f32),
@@ -584,6 +638,9 @@
         dma((8,)),
         dma((4,)),
         dma((4,)),
+        dma((11,)),
+        dma((2,)),
+        pltpu.SemaphoreType.REGULAR,
     ]
     residuals, gradients = pl.pallas_call(
         functools.partial(kernel, ngx, ngy, npart),
@@ -591,8 +648,8 @@
             jax.ShapeDtypeStruct(observed_data.shape, f32),
             jax.ShapeDtypeStruct((32, 128), f32),
         ),
-        in_specs=[vmem] * 11,
-        out_specs=(vmem, vmem),
+        in_specs=[anywhere] * 11,
+        out_specs=(anywhere, anywhere),
         scratch_shapes=scratch,
         compiler_params=pltpu.CompilerParams(collective_id=0, has_side_effects=True),
         name="window",

time: 70.8 us -> 64.2 us (0.907)
  Pallas kernels: 67.9 us -> 61.3 us
    pallas_call x1, Pallas kernels: 67.9 us -> 61.3 us  [shards(): pl.pallas_call(functools.partial(kernel, ngx, ngy, npart), out_shape=(jax...]
where the time goes in v2:
time: 64.2 us; the launch traced here: 63.9 us
  Pallas kernels  61.3 us (95%)
  local copies, waits for them, and re-layouts  1.94 us (3%)
  between operations  0.65 us (1%)
    pallas_call x1, Pallas kernels, shards(): pl.pallas_call(functools.partial(kernel, ngx, ngy, npart), out_shape=(jax...  61.3 us
    unnamed x4, local copies, waits for them, and re-layouts  1.94 us

profile of v2, /device:TPU:1, one launch (start us, length us, event | category | flops | bytes accessed | tf_op | source)
XLA Modules:
  0.0 63.9 jit_solution(1689231141108512142)
XLA Ops:
  0.6 61.3 %window.1 = (f32[3,1024]{1,0:T(4,128)}, f32[32,128]{1,0:T(8,128)}) custom-call(f32[144,128]{1,0:T(8,128)} %bitcast.9, f32[16,128]{1,0:T(8,128)} %bitcast.11, f32[16,128]{1,0:T(8,128)} %bitcast.12, f32[16,128]{1,0:T(8,128)} %bitcast.13, s32[1,64]{1,0:T(1,128)} %bitcast.17, f32[3,64]{1,0:T(4,128)} %swave_in.1, s32[16,128]{1,0:T(8,128)} %bitcast.14, ...), custom_call_target="tpu_custom_call" | custom-call | tf_op jit(solution)/shard_map/window/pallas_call | solution.py:645
  62.0 0.0 copy-start
  62.0 1.3 %copy.15 = f32[3,1024]{1,0:T(4,128)} copy(f32[3,1024]{1,0:T(4,128)} %get-tuple-element.8) | data formatting | bytes 24576
  63.3 0.0 copy-done
  63.3 0.6 copy.16
Async XLA Ops:
  62.0 1.3 %copy-start = (f32[32,128]{1,0:T(8,128)S(1)}, f32[32,128]{1,0:T(8,128)}, u32[]{:S(2)}) copy-start(f32[32,128]{1,0:T(8,128)} %get-tuple-element.5) | copy-start | bytes 49156

commit v3 on v2

--- a/solution.py
+++ b/solution.py
@@ -46,6 +46,19 @@
 
 def ones_where(mask):
     return jnp.where(mask, 1.0, 0.0).astype(jnp.bfloat16)
+
+
+def narrow(x):
+    return x.astype(jnp.float32).astype(jnp.bfloat16)
+
+
+def spread_rows(x, key_rows, key, copies):
+    hit = key_rows == narrow(key)
+    zero = jnp.zeros(hit.shape, jnp.bfloat16)
+    pieces = split(jnp.concatenate([x, x], axis=0))
+    return jnp.concatenate(
+        [jnp.where(hit, jnp.concatenate([piece] * copies, axis=0), zero) for piece in pieces], axis=0
+    )
 
 
 def ahead(f, axis):
@@ -394,6 +407,7 @@
 
     width = 2 if nchunk % 2 == 0 else 1
     wide = 128 * width
+    by_four, by_eight = narrow(iota((128, wide), 0) >> 2), narrow(iota((128, wide), 0) >> 3)
     gpieces = jnp.concatenate(split(glhs[...]), axis=0)
     acc = jnp.zeros((PIECES * 128, 128), jnp.float32)
     for c in range(0, nchunk, width):
@@ -412,12 +426,7 @@
         picked = jnp.where((sub_of(wide) & 3) == 3, chan_c.astype(jnp.float32), picked)
         own_c, rank_c = chunk_key(c, width)
         key_c = (own_c >> gy_bits) * 2 + (rank_c >> 1)
-        hit = (iota((128, wide), 0) >> 2) == key_c
-        parts = [
-            jnp.where(hit, jnp.concatenate([part.astype(jnp.float32)] * 16, axis=0), 0.0).astype(jnp.bfloat16)
-            for part in split(picked)
-        ]
-        acc = acc + dot(jnp.concatenate(parts, axis=0), lane1h[:, lanes], NT)
+        acc = acc + dot(spread_rows(picked, by_four, key_c, 8), lane1h[:, lanes], NT)
     total = acc[0:128]
     for i in range(1, PIECES):
         total = total + acc[128 * i : 128 * i + 128]
@@ -454,21 +463,19 @@
 
     acc = jnp.zeros((PIECES * 32, 128), jnp.float32)
     sub256 = sub_of(256) >> 2
+    rows256 = narrow(iota((128, 256), 0))
+    one, none = jnp.ones((128, 256), jnp.bfloat16), jnp.zeros((128, 256), jnp.bfloat16)
+    by_four32 = narrow(iota((32, 256), 0) >> 2)
     for d in range(16):
         tile = arr[8 * d : 8 * d + 8, :]
         turned = pltpu.roll(tile, 4, 0)
         both = jnp.concatenate([jnp.where(sub < 4, tile, turned), jnp.where(sub < 4, turned, tile)], axis=1)
         ids = both[3:4, :].astype(jnp.int32)
-        onehot = ones_where(iota((128, 256), 0) == (ids & 127))
+        onehot = jnp.where(rows256 == narrow(ids & 127), one, none)
         chan1h[:, 256 * d : 256 * d + 256] = onehot
         hi = ids >> 7
         hirow[d : d + 1, :] = hi
-        parts = []
-        for part in split(both):
-            part = part.astype(jnp.float32)
-            for j in range(4):
-                parts.append(jnp.where(hi == sub256 + 2 * j, part, 0.0).astype(jnp.bfloat16))
-        acc = acc + dot(jnp.concatenate(parts, axis=0), onehot, NT)
+        acc = acc + dot(spread_rows(both, by_four32, hi, 2), onehot, NT)
     sums = acc[0:32]
     for i in range(1, PIECES):
         sums = sums + acc[32 * i : 32 * i + 32]
@@ -511,12 +518,7 @@
             picked = picked + jnp.where(key_c == half + 2 * r, tile, 0.0)
         picked = (picked + pltpu.roll(picked, 4, 0)) * weights(c, width)
         _, row_c = row_of(c, width)
-        hit = (iota((128, wide), 0) >> 3) == row_c
-        parts = [
-            jnp.where(hit, jnp.concatenate([part.astype(jnp.float32)] * 16, axis=0), 0.0).astype(jnp.bfloat16)
-            for part in split(picked)
-        ]
-        acc = acc + dot(jnp.concatenate(parts, axis=0), win[:, lanes], NT)
+        acc = acc + dot(spread_rows(picked, by_eight, row_c, 8), win[:, lanes], NT)
     total = acc[0:128]
     for i in range(1, PIECES):
         total = total + acc[128 * i : 128 * i + 128]
@@ -569,6 +571,17 @@
     put_grad.start()
     put_res.wait()
     put_grad.wait()
+
+
+def publish(res_in, grad_in, res_out, grad_out, sem):
+    copies = [
+        pltpu.make_async_copy(res_in, res_out, sem.at[0]),
+        pltpu.make_async_copy(grad_in, grad_out, sem.at[1]),
+    ]
+    for copy in copies:
+        copy.start()
+    for copy in copies:
+        copy.wait()
 
 
 def shards(
@@ -651,9 +664,10 @@
         in_specs=[anywhere] * 11,
         out_specs=(anywhere, anywhere),
         scratch_shapes=scratch,
-        compiler_params=pltpu.CompilerParams(collective_id=0, has_side_effects=True),
+        compiler_params=pltpu.CompilerParams(collective_id=0, has_side_effects=True, vmem_limit_bytes=25165824),
         name="window",
     )(
+        *[pltpu.with_memory_space_constraint(x, pltpu.HBM) for x in (
         initial_state.reshape(144, 128),
         lame_lambda.reshape(16, 128),
         shear_modulus.reshape(16, 128),
@@ -664,8 +678,17 @@
         segment_weight,
         partial_owner.reshape(-1, 128),
         partial_channel.reshape(-1, 128),
-        observed_data,
+        observed_data)],
     )
+    residuals, gradients = pl.pallas_call(
+        publish,
+        out_shape=(jax.ShapeDtypeStruct(observed_data.shape, f32), jax.ShapeDtypeStruct((32, 128), f32)),
+        in_specs=[anywhere, anywhere],
+        out_specs=(anywhere, anywhere),
+        scratch_shapes=[dma((2,))],
+        compiler_params=pltpu.CompilerParams(vmem_limit_bytes=1 << 20),
+        name="publish",
+    )(residuals, gradients)
     return residuals, gradients.reshape(2, 4, 4, 128)
 
 

time: 64.2 us -> 62.5 us (0.974)
  local copies, waits for them, and re-layouts: 1.94 us -> 0 us
    unnamed x4 -> x0, local copies, waits for them, and re-layouts: 1.94 us -> none
where the time goes in v3:
time: 62.5 us; the launch traced here: 62.3 us
  Pallas kernels  61.7 us (99%)
  between operations  0.64 us (1%)
    pallas_call x1, Pallas kernels, shards(): pl.pallas_call(functools.partial(kernel, ngx, ngy, npart), out_shape=(jax...  61.1 us

profile of v3, /device:TPU:1, one launch (start us, length us, event | category | flops | bytes accessed | tf_op | source)
XLA Modules:
  0.0 62.3 jit_solution(10988890497307036473)
XLA Ops:
  0.6 61.1 %window.1 = (f32[3,1024]{1,0:T(4,128)S(1)}, f32[32,128]{1,0:T(8,128)S(1)}) custom-call(f32[144,128]{1,0:T(8,128)} %bitcast.9, f32[16,128]{1,0:T(8,128)} %bitcast.10, f32[16,128]{1,0:T(8,128)} %bitcast.11, f32[16,128]{1,0:T(8,128)} %bitcast.12, s32[1,64]{1,0:T(1,128)} %bitcast.16, f32[3,64]{1,0:T(4,128)} %swave_in.1, s32[16,128]{1,0:T(8,128)} %bitcast.13, ...), custom_call_target="tpu_custom_call" | custom-call | tf_op jit(solution)/shard_map/window/pallas_call | solution.py:658
  61.7 0.6 %publish.1 = (f32[3,1024]{1,0:T(4,128)}, f32[32,128]{1,0:T(8,128)}) custom-call(f32[3,1024]{1,0:T(4,128)S(1)} %get-tuple-element.6.res_in, f32[32,128]{1,0:T(8,128)S(1)} %get-tuple-element.7.grad_in), custom_call_target="tpu_custom_call" | custom-call | tf_op jit(solution)/shard_map/publish/pallas_call | solution.py:683

commit v4 on v3

--- a/solution.py
+++ b/solution.py
@@ -129,8 +129,6 @@
     owner,
     chan,
     obs,
-    res,
-    grad,
     own,
     xr,
     strip,
@@ -170,7 +168,6 @@
     esend,
     erecv,
     isem,
-    osem,
     ready,
 ):
     gx, gy = lax.axis_index("gx"), lax.axis_index("gy")
@@ -236,7 +233,7 @@
     exl[...] = jnp.zeros_like(exl)
     glhs[...] = jnp.zeros_like(glhs)
     obs32[...] = jnp.zeros_like(obs32)
-    for read in reads[:6]:
+    for read in reads[:7]:
         read.wait()
 
     cell = scell[...]
@@ -269,6 +266,26 @@
 
     pack(lambda i: own[8 * i : 8 * i + 8, :], 2 * NF, put_strip)
 
+    ownf = owner[...].astype(jnp.float32)
+    cols = jnp.concatenate([ownf, jnp.zeros((128 - nchunk, 128), jnp.float32)], axis=0).T
+    for c in range(nchunk):
+        colb[c] = jnp.broadcast_to(cols[:, c : c + 1], (128, 128))
+    earlier = iota((128, 128), 0) < iota((128, 128), 1)
+
+    def rank_chunk(c):
+        row = jnp.broadcast_to(owner[pl.ds(c, 1), :].astype(jnp.float32), (128, 128))
+        same = jnp.where((colb[c] == row) & earlier, 1.0, 0.0)
+
+        def more(q, count):
+            hit = jnp.where(colb[q] == row, 1.0, 0.0)
+            return count + hit.reshape(16, 8, 128).sum(axis=0)
+
+        count = lax.fori_loop(0, c, more, same.reshape(16, 8, 128).sum(axis=0))
+        rank[pl.ds(c, 1), :] = jnp.sum(count, axis=0, keepdims=True)
+
+    halfway = nchunk * 11 // 16
+    pl.loop(0, halfway)(rank_chunk)
+
     pl.semaphore_wait(barrier, len(greeted))
     for i in far_first(nx):
         x, y = peer_x(i)
@@ -276,14 +293,14 @@
 
     def halo_copies(rows, rows_to, strips, strips_to, send, recv):
         plan = [
-            (rows, rows_to.at[0], right_x, gy),
-            (rows, rows_to.at[1], left_x, gy),
-            (strips.at[0], strips_to.at[1, 0], gx, right_y),
-            (strips.at[1], strips_to.at[1, 1], gx, left_y),
             (strips.at[0], strips_to.at[0, 0], right_x, right_y),
             (strips.at[1], strips_to.at[0, 1], right_x, left_y),
             (strips.at[0], strips_to.at[2, 0], left_x, right_y),
             (strips.at[1], strips_to.at[2, 1], left_x, left_y),
+            (strips.at[0], strips_to.at[1, 0], gx, right_y),
+            (strips.at[1], strips_to.at[1, 1], gx, left_y),
+            (rows, rows_to.at[0], right_x, gy),
+            (rows, rows_to.at[1], left_x, gy),
         ]
         copies = [
             pltpu.make_async_remote_copy(
@@ -301,26 +318,10 @@
         return copies
 
     copies = halo_copies(own, xr, strip, yr, hsend, hrecv)
-    for read in reads[6:]:
+    for read in reads[7:]:
         read.wait()
 
-    ownf = owner[...].astype(jnp.float32)
-    cols = jnp.concatenate([ownf, jnp.zeros((128 - nchunk, 128), jnp.float32)], axis=0).T
-    for c in range(nchunk):
-        colb[c] = jnp.broadcast_to(cols[:, c : c + 1], (128, 128))
-    earlier = iota((128, 128), 0) < iota((128, 128), 1)
-
-    @pl.loop(0, nchunk)
-    def _(c):
-        row = jnp.broadcast_to(owner[pl.ds(c, 1), :].astype(jnp.float32), (128, 128))
-        same = jnp.where((colb[c] == row) & earlier, 1.0, 0.0)
-
-        def more(q, count):
-            hit = jnp.where(colb[q] == row, 1.0, 0.0)
-            return count + hit.reshape(16, 8, 128).sum(axis=0)
-
-        count = lax.fori_loop(0, c, more, same.reshape(16, 8, 128).sum(axis=0))
-        rank[pl.ds(c, 1), :] = jnp.sum(count, axis=0, keepdims=True)
+    pl.loop(halfway, nchunk)(rank_chunk)
 
     for i in range(8):
         obs32[4 * i : 4 * i + 3, :] = obs[:, 128 * i : 128 * i + 128]
@@ -481,9 +482,7 @@
         sums = sums + acc[32 * i : 32 * i + 32]
     sums = jnp.where((iota((32, 128), 0) & 3) == 3, 0.0, sums - obs32[...])
     for i in range(8):
-        res[:, 128 * i : 128 * i + 128] = sums[4 * i : 4 * i + 3, :]
-    put_res = pltpu.make_async_copy(res, res_out, osem.at[0])
-    put_res.start()
+        res_out[:, 128 * i : 128 * i + 128] = sums[4 * i : 4 * i + 3, :]
 
     pieces = jnp.concatenate(split(sums), axis=0)
     for d in range(16):
@@ -530,22 +529,30 @@
     pack(lambda i: load[8 * i : 8 * i + 8, :], 16, put_strip2)
     copies = halo_copies(load, xr2, strip2, yr2, h2send, h2recv)
     ext[...] = jnp.zeros_like(ext)
+
+    def place_loads(g, ref, drop):
+        for f in range(2):
+            for t in range(STEPS):
+                for z in range(4):
+                    part = ref[pl.ds(32 * z + 4 * f + t, 4, stride=8), :]
+                    if drop is not None:
+                        part = jnp.where(drop, 0.0, part)
+                    exl[2 * t + f, 16 * z + 4 * g : 16 * z + 4 * g + 4, 0:128] = part
+
+    place_loads(1, load, None)
     for copy in copies:
         copy.wait()
+    place_loads(0, xr2.at[0], first_x)
+    place_loads(2, xr2.at[1], last_x)
     for g in range(3):
         both = comb(yr2, g, 0)
         for k in range(16):
             halo2[g, pl.ds(8 * k, 8), :] = pltpu.roll(both, (124 - 8 * k) % 128, 1)
-    sources = ((xr2.at[0], first_x), (load, None), (xr2.at[1], last_x))
     for f in range(2):
         for t in range(STEPS):
             for z in range(4):
                 rows = pl.ds(32 * z + 4 * f + t, 4, stride=8)
-                for g, (ref, drop) in enumerate(sources):
-                    part = ref[rows, :]
-                    if drop is not None:
-                        part = jnp.where(drop, 0.0, part)
-                    exl[2 * t + f, 16 * z + 4 * g : 16 * z + 4 * g + 4, 0:128] = part
+                for g in range(3):
                     exl[2 * t + f, 16 * z + 4 * g : 16 * z + 4 * g + 4, 128:256] = halo2[g, rows, :]
 
     lam_grad = jnp.zeros((16, 128), jnp.float32)
@@ -565,12 +572,8 @@
         prod = [a * b for a, b in zip(fwd, adj)]
         lam_grad = lam_grad + (fwd[0] + fwd[1] + fwd[2]) * (adj[0] + adj[1] + adj[2])
         mu_grad = mu_grad + (2.0 * (prod[0] + prod[1] + prod[2]) + prod[3] + prod[4] + prod[5])
-    grad[0:16, :] = lam_grad
-    grad[16:32, :] = mu_grad
-    put_grad = pltpu.make_async_copy(grad, grad_out, osem.at[1])
-    put_grad.start()
-    put_res.wait()
-    put_grad.wait()
+    grad_out[0:16, :] = lam_grad
+    grad_out[16:32, :] = mu_grad
 
 
 def publish(res_in, grad_in, res_out, grad_out, sem):
@@ -611,8 +614,6 @@
         pltpu.VMEM((npart // 128, 128), jnp.int32),
         pltpu.VMEM((npart // 128, 128), jnp.int32),
         pltpu.VMEM(observed_data.shape, f32),
-        pltpu.VMEM(observed_data.shape, f32),
-        pltpu.VMEM((32, 128), f32),
         pltpu.VMEM((16 * NF, 128), f32),
         pltpu.VMEM((2, 16 * NF, 128), f32),
         pltpu.VMEM((2, 16, 128), f32),
@@ -652,7 +653,6 @@
         dma((4,)),
         dma((4,)),
         dma((11,)),
-        dma((2,)),
         pltpu.SemaphoreType.REGULAR,
     ]
     residuals, gradients = pl.pallas_call(
@@ -662,7 +662,7 @@
             jax.ShapeDtypeStruct((32, 128), f32),
         ),
         in_specs=[anywhere] * 11,
-        out_specs=(anywhere, anywhere),
+        out_specs=(pl.BlockSpec(memory_space=pltpu.VMEM),) * 2,
         scratch_shapes=scratch,
         compiler_params=pltpu.CompilerParams(collective_id=0, has_side_effects=True, vmem_limit_bytes=25165824),
         name="window",

time: 62.5 us -> 62.5 us (level)
  no operation moved by 1% of the time
where the time goes in v4:
time: 62.5 us; the launch traced here: 62.3 us
  Pallas kernels  61.7 us (99%)
  between operations  0.64 us (1%)
    pallas_call x1, Pallas kernels, shards(): pl.pallas_call(functools.partial(kernel, ngx, ngy, npart), out_shape=(jax...  61.1 us

profile of v4, /device:TPU:1, one launch (start us, length us, event | category | flops | bytes accessed | tf_op | source)
XLA Modules:
  0.0 62.3 jit_solution(8569285517256588550)
XLA Ops:
  0.6 61.1 %window.1 = (f32[3,1024]{1,0:T(4,128)S(1)}, f32[32,128]{1,0:T(8,128)S(1)}) custom-call(f32[144,128]{1,0:T(8,128)} %bitcast.9, f32[16,128]{1,0:T(8,128)} %bitcast.10, f32[16,128]{1,0:T(8,128)} %bitcast.11, f32[16,128]{1,0:T(8,128)} %bitcast.12, s32[1,64]{1,0:T(1,128)} %bitcast.16, f32[3,64]{1,0:T(4,128)} %swave_in.1, s32[16,128]{1,0:T(8,128)} %bitcast.13, ...), custom_call_target="tpu_custom_call" | custom-call | tf_op jit(solution)/shard_map/window/pallas_call | solution.py:658
  61.7 0.6 %publish.1 = (f32[3,1024]{1,0:T(4,128)}, f32[32,128]{1,0:T(8,128)}) custom-call(f32[3,1024]{1,0:T(4,128)S(1)} %get-tuple-element.6.res_in, f32[32,128]{1,0:T(8,128)S(1)} %get-tuple-element.7.grad_in), custom_call_target="tpu_custom_call" | custom-call | tf_op jit(solution)/shard_map/publish/pallas_call | solution.py:683

commit v5 on v4

--- a/solution.py
+++ b/solution.py
@@ -103,6 +103,35 @@
             ext[f, pl.ds(16 * z, 16), :] = plane(ext, f, z) + DT * (dil + 2.0 * mu * e)
         for f, e in ((6, exy), (7, exz), (8, eyz)):
             ext[f, pl.ds(16 * z, 16), :] = plane(ext, f, z) + DT * mu * e
+
+
+def first_step(ext, mats, load_x, load_y, emit):
+    def plane(ref, f, z):
+        return ref[f, pl.ds(16 * z, 16), :]
+
+    none = jnp.zeros((16, 256), jnp.float32)
+    for z in range(4):
+        rows = pl.ds(16 * z, 16)
+        scale = DT * plane(mats, 0, z)
+        ext[0, rows, :] = scale * ahead(load_x[rows, :], 0)
+        ext[1, rows, :] = scale * ahead(load_y[rows, :], 1)
+        ext[2, rows, :] = none
+    for z in range(4):
+        rows = pl.ds(16 * z, 16)
+        vx, vy = plane(ext, 0, z), plane(ext, 1, z)
+        exx = behind(vx, 0)
+        eyy = behind(vy, 1)
+        exy = ahead(vx, 1) + ahead(vy, 0)
+        exz = (plane(ext, 0, z + 1) if z < 3 else 0.0) - vx
+        eyz = (plane(ext, 1, z + 1) if z < 3 else 0.0) - vy
+        emit(z, [e[4:8, 0:128] for e in (exx, eyy, none, exy, exz, eyz)])
+        lam, mu = plane(mats, 1, z), plane(mats, 2, z)
+        dil = lam * (exx + eyy)
+        ext[3, rows, :] = load_x[rows, :] + DT * (dil + 2.0 * mu * exx)
+        ext[4, rows, :] = load_y[rows, :] + DT * (dil + 2.0 * mu * eyy)
+        ext[5, rows, :] = DT * dil
+        for f, e in ((6, exy), (7, exz), (8, eyz)):
+            ext[f, rows, :] = DT * mu * e
 
 
 def kernel(
@@ -528,7 +557,6 @@
 
     pack(lambda i: load[8 * i : 8 * i + 8, :], 16, put_strip2)
     copies = halo_copies(load, xr2, strip2, yr2, h2send, h2recv)
-    ext[...] = jnp.zeros_like(ext)
 
     def place_loads(g, ref, drop):
         for f in range(2):
@@ -559,14 +587,17 @@
     mu_grad = jnp.zeros((16, 128), jnp.float32)
     for k in range(STEPS):
         t = STEPS - 1 - k
-        for f in range(2):
-            ext[3 + f] = ext[3 + f] + exl[2 * t + f]
 
         def emit(z, e):
             for i in range(6):
                 ad[i, pl.ds(4 * z, 4), :] = e[i]
 
-        time_step(ext, mats, emit)
+        if k == 0:
+            first_step(ext, mats, exl.at[2 * t], exl.at[2 * t + 1], emit)
+        else:
+            for f in range(2):
+                ext[3 + f] = ext[3 + f] + exl[2 * t + f]
+            time_step(ext, mats, emit)
         fwd = [es[6 * t + i] for i in range(6)]
         adj = [ad[i] for i in range(6)]
         prod = [a * b for a, b in zip(fwd, adj)]

time: 62.5 us -> 62.4 us (level)
  no operation moved by 1% of the time
where the time goes in v5:
time: 62.4 us; the launch traced here: 62.2 us
  Pallas kernels  61.6 us (99%)
  between operations  0.64 us (1%)
    pallas_call x1, Pallas kernels, shards(): pl.pallas_call(functools.partial(kernel, ngx, ngy, npart), out_shape=(jax...  61 us

profile of v5, /device:TPU:1, one launch (start us, length us, event | category | flops | bytes accessed | tf_op | source)
XLA Modules:
  0.0 62.2 jit_solution(606264763239039280)
XLA Ops:
  0.6 61.0 %window.1 = (f32[3,1024]{1,0:T(4,128)S(1)}, f32[32,128]{1,0:T(8,128)S(1)}) custom-call(f32[144,128]{1,0:T(8,128)} %bitcast.9, f32[16,128]{1,0:T(8,128)} %bitcast.10, f32[16,128]{1,0:T(8,128)} %bitcast.11, f32[16,128]{1,0:T(8,128)} %bitcast.12, s32[1,64]{1,0:T(1,128)} %bitcast.16, f32[3,64]{1,0:T(4,128)} %swave_in.1, s32[16,128]{1,0:T(8,128)} %bitcast.13, ...), custom_call_target="tpu_custom_call" | custom-call | tf_op jit(solution)/shard_map/window/pallas_call | solution.py:689
  61.6 0.6 %publish.1 = (f32[3,1024]{1,0:T(4,128)}, f32[32,128]{1,0:T(8,128)}) custom-call(f32[3,1024]{1,0:T(4,128)S(1)} %get-tuple-element.6.res_in, f32[32,128]{1,0:T(8,128)S(1)} %get-tuple-element.7.grad_in), custom_call_target="tpu_custom_call" | custom-call | tf_op jit(solution)/shard_map/publish/pallas_call | solution.py:714
